TPU v7x, 32 devices: a whole 2x2x4 slice. The times are simulated.
32 devices in a mesh: gx: 4 (over z), gy: 4 (over y, x), gz: 2 (over core).
Axes of the slice: x: 2, y: 2, z: 4, core: 2. Of those that a mesh axis runs over, the one named last changes fastest.
Arguments:
- forcing: float32 [3, 64, 64, 256], P(None, 'gx', 'gy', 'gz'), may hold values from -6 to 6
- start_field: float32 [3, 64, 64, 256], P(None, 'gx', 'gy', 'gz'), may hold values from -6 to 6
- modulus: float32 [64, 64, 256], P('gx', 'gy', 'gz'), may hold values from 1 to 4
- corners: int32 [32, 3], P(('gx', 'gy', 'gz')), may hold values from 0 to 236, as said below
Outputs:
- displacement: float32 [3, 64, 64, 256], P(None, 'gx', 'gy', 'gz')
- new_modulus: float32 [64, 64, 256], P('gx', 'gy', 'gz')
Inputs may be any that keep to these rules, and one draw needn't show every extreme that they name: `corners`: subzone i is handled by device i // 1 in row-major order over (gx, gy, gz). In each dimension its corner lies within lo - 5 to lo + B + 5 - 2 * 10, where lo and B are that device's first voxel and voxel count in that dimension, and the subzone lies inside the grid.
All inputs are finite; a program needn't handle non-finite values.
Results may differ from a plain program's by a relative error of at most 0.0003.
Values sent between devices are 32-bit elements; how exact they have to be, the bound alone decides.
A program may use at most 192 MiB of HBM per device.

v0:
```python
import functools
import math

import jax
import jax.numpy as jnp
from jax import lax
from jax.experimental import pallas as pl
from jax.experimental.pallas import tpu as pltpu
from jax.sharding import PartitionSpec as P

PC = 10
HALO = 6
FSWEEPS = 4


MASS_TERM = 0.5
DAMPING = 0.1
EPSILON = 1e-06
HIGHEST = lax.Precision.HIGHEST
PANEL = 2
F32 = jnp.float32


def extended(block, sides, width):
    for axis, dim in sides:
        count = lax.axis_size(axis)
        forward = [(i, i + 1) for i in range(count - 1)]
        backward = [(target, source) for source, target in forward]
        low = lax.ppermute(
            lax.slice_in_dim(block, block.shape[dim] - width, None, axis=dim), axis, forward
        )
        high = lax.ppermute(lax.slice_in_dim(block, 0, width, axis=dim), axis, backward)
        block = jnp.concatenate([low, block, high], axis=dim)
    return block


def pack_margins(values, which_axis, margin):
    inner = values.shape[which_axis] - 2 * margin
    return jnp.concatenate(
        [
            lax.slice_in_dim(values, 0, margin, axis=which_axis),
            lax.slice_in_dim(values, 2 * margin, inner, axis=which_axis),
            lax.slice_in_dim(values, inner + margin, inner + 2 * margin, axis=which_axis),
        ],
        axis=which_axis,
    )


def fold_margins(values, received, which_axis, margin):
    inner = values.shape[which_axis] - 2 * margin
    middle_shape = list(values.shape)
    middle_shape[which_axis] = inner - 2 * margin
    added = jnp.concatenate(
        [
            lax.slice_in_dim(received, 0, margin, axis=which_axis),
            jnp.zeros(middle_shape, jnp.float32),
            lax.slice_in_dim(received, inner + margin, inner + 2 * margin, axis=which_axis),
        ],
        axis=which_axis,
    )
    return lax.slice_in_dim(values, margin, inner + margin, axis=which_axis) + added


def dot(a, b, contract):
    return lax.dot_general(
        a, b, ((contract[:1], contract[1:]), ((), ())), precision=HIGHEST, preferred_element_type=F32
    )


def roll(values, shift, axis):
    return pltpu.roll(values, shift % values.shape[axis], axis)


def iota(shape, axis):
    return lax.broadcasted_iota(jnp.int32, shape, axis)


def relax_planes(totals, brick, margin, wide, field_out, buffers, faces):
    _, span_x, rows, lanes = wide.shape
    mx, my, mz, inverse = faces
    low = [lax.axis_index(name) * size - margin for name, size in zip(("gx", "gy", "gz"), brick)]
    y_pos = low[1] + iota((rows, lanes), 0)
    lane = iota((rows, lanes), 1)
    z_pos = low[2] + margin + jnp.where(lane < brick[2] + 64, lane, lane - lanes)
    inside = (y_pos >= 0) & (y_pos < totals[1]) & (z_pos >= 0) & (z_pos < totals[2])

    mx[0] = 0.5 * (wide[6, 0] + wide[6, 1])

    def couple(x, _):
        m = wide[6, x]
        face_z = 0.5 * (m + roll(m, -1, 1))
        face_y = 0.5 * (m + roll(m, -1, 0))
        face_x = 0.5 * (m + wide[6, x + 1])
        mx[x], my[x], mz[x] = face_x, face_y, face_z
        below = MASS_TERM + face_x + mx[x - 1] + face_y + roll(face_y, 1, 0)
        below = below + face_z + roll(face_z, 1, 1)
        x_pos = low[0] + x
        here = inside & (x_pos >= 0) & (x_pos < totals[0])
        inverse[x] = jnp.where(here, 1.0 / below, 0.0)
        return 0

    lax.fori_loop(1, span_x - 1, couple, 0)
    source = wide
    for sweep in range(FSWEEPS):
        target = buffers[sweep % 2]

        def relax(x, _, source=source, target=target):
            face_x, face_y, face_z, before = mx[x], my[x], mz[x], mx[x - 1]
            scale = inverse[x]
            for k in range(3):
                u = source[k, x]
                total = wide[3 + k, x] + face_x * source[k, x + 1] + before * source[k, x - 1]
                total = total + face_y * roll(u, -1, 0) + roll(face_y * u, 1, 0)
                total = total + face_z * roll(u, -1, 1) + roll(face_z * u, 1, 1)
                target[k, x] = total * scale
            return 0

        lax.fori_loop(sweep + 1, span_x - 1 - sweep, relax, 0)
        source = target
    for k in range(3):
        for x in range(brick[0]):
            field_out[k, x] = source[k, margin + x, margin : margin + brick[1], : brick[2]]
    return source


def cut_zone(begin, margin, source, wide, zone_u, zone_f, zone_m):
    count, rows = zone_m.shape[:2]
    shift = lax.rem(source.shape[-1] + margin - begin[2], source.shape[-1])
    shift_y = lax.rem(source.shape[-2] - begin[1], source.shape[-2])

    def cut(x, _):
        def take(ref, k):
            plane = pltpu.roll(ref[k, begin[0] + x], shift, 1)[:, :128]
            return pltpu.roll(plane, shift_y, 0)[:rows]

        for k in range(3):
            zone_u[k, x] = take(source, k)
            zone_f[k, x] = take(wide, 3 + k)
        zone_m[x] = take(wide, 6)
        return 0

    lax.fori_loop(0, count, cut, 0)


FIELDS = 8


def coarse_fields(zone_u, zone_f, zone_m, temp, fields):
    rows = zone_m.shape[1]
    first_y = iota((rows, 128), 0) % 2 == 1
    first_z = iota((rows, 128), 1) % 2 == 1
    rank = iota((PC, 128), 0)
    lane = iota((PC, 128), 1)
    for x in range(PC):
        for k in range(3):
            sums = [None] * FIELDS

            def put(number, value):
                sums[number] = value if sums[number] is None else sums[number] + value

            for a in range(2):
                at = 2 * x + 1 + a
                u, m = zone_u[k, at], zone_m[at]
                applied = MASS_TERM * u
                laplace = jnp.zeros_like(u)
                for number, (axis, step) in enumerate(
                    ((0, 1), (0, -1), (1, 1), (1, -1), (2, 1), (2, -1))
                ):
                    if axis == 0:
                        u_next, m_next = zone_u[k, at + step], zone_m[at + step]
                    else:
                        u_next, m_next = roll(u, -step, axis - 1), roll(m, -step, axis - 1)
                    change = u - u_next
                    applied = applied + 0.5 * (m + m_next) * change
                    laplace = laplace + change
                    flow = -0.5 * m_next * change
                    if axis == 0:
                        same = (a == 0) == (step == 1)
                        put(0 if same else 1 + number, flow)
                    else:
                        first = first_y if axis == 1 else first_z
                        near = first if step == 1 else ~first
                        put(0, jnp.where(near, flow, 0.0))
                        put(1 + number, jnp.where(near, 0.0, flow))
                put(0, -0.5 * m * laplace)
                put(7, zone_f[k, at] - applied)
            for number in range(FIELDS):
                slot = temp.at[k * FIELDS + number]
                slot[...] = sums[number]
                pair = slot[pl.ds(1, PC, stride=2), :] + slot[pl.ds(2, PC, stride=2), :]
                pair = pair + roll(pair, -1, 1)
                keep = (lane % 2 == 1) & (lane < 2 * PC)
                if number == 1 and x == PC - 1 or number == 2 and x == 0:
                    keep = jnp.zeros_like(keep)
                if number == 3:
                    keep = keep & (rank < PC - 1)
                if number == 4:
                    keep = keep & (rank > 0)
                if number == 5:
                    keep = keep & (lane < 2 * PC - 2)
                if number == 6:
                    keep = keep & (lane > 1)
                fields[k * FIELDS + number, x * PC : (x + 1) * PC, :] = jnp.where(keep, pair, 0.0)


def assemble(fields, strip, mat, side):
    size = fields.shape[1]
    gap = iota((size, 128), 1) - iota((size, 128), 0)
    mat[...] = jnp.zeros_like(mat)
    side[...] = jnp.zeros_like(side)
    for c in range(2):
        for t in range(PC // 2):
            z = t if c == 0 else PC - 1 - t
            for k in range(3):
                def column(number):
                    value = fields[k * FIELDS + number, :, 2 * z + 1 : 2 * z + 2]
                    return jnp.broadcast_to(value, (size, 128))

                part = slice(k * size, (k + 1) * size)
                ahead, behind = (5, 6) if c == 0 else (6, 5)
                strip[part, 0:128] = jnp.where(gap == 0, column(behind), 0.0)
                inner = jnp.where(gap == 0, column(0), 0.0)
                for number, offset in ((1, PC), (2, -PC), (3, 1), (4, -1)):
                    inner = jnp.where(gap == offset, column(number), inner)
                strip[part, 128:256] = inner
                strip[part, 256:384] = jnp.where(gap == 0, column(ahead), 0.0)
                strip[part, 384:512] = column(7)
            product = dot(strip[:, :384], strip[...], (0, 0))
            for i in range(3):
                at = t - 1 + i
                if at < 0:
                    continue
                rows = slice(128 * i, 128 * (i + 1))
                mat[c, at] += product[rows, 128 * i : 128 * (i + 1)]
                for j in range(i + 1, 3):
                    place = slice(128 * (j - i - 1), 128 * (j - i))
                    side[c, at, :, place] += product[rows, 128 * j : 128 * (j + 1)]
                side[c, at, :, 256:384] += product[rows, 384:512]


def inverted(blocks, count):
    row_at = iota(blocks[0].shape, 0)
    lane_at = iota((1, blocks[0].shape[1]), 1)
    shape = blocks[0].shape
    for first in range(0, count, PANEL):
        pivots = range(first, min(first + PANEL, count))
        states = []
        for block in blocks:
            columns = [jnp.broadcast_to(block[:, j : j + 1], shape) for j in pivots]
            states.append([columns, [block[j : j + 1, :] for j in pivots], block])
        for i, j in enumerate(pivots):
            for state in states:
                columns, rows, block = state
                pivot = 1.0 / columns[i][j : j + 1, :]
                row = jnp.where(lane_at == j, pivot, rows[i] * pivot)
                column = jnp.where(row_at == j, -1.0, columns[i])
                for n in range(i + 1, len(columns)):
                    crossing = columns[n][j : j + 1, :] * pivot
                    rows[n] = jnp.where(lane_at == j, 0.0, rows[n])
                    rows[n] = rows[n] - columns[i][pivots[n] : pivots[n] + 1, :] * row
                    columns[n] = jnp.where(row_at == j, 0.0, columns[n]) - column * crossing
                clear = (row_at == j) | (lane_at == j)
                state[2] = jnp.where(clear, 0.0, block) - column * row
        blocks = [state[2] for state in states]
    return blocks


def eliminate(t, chains, size, ridge, mat, side, solved):
    params = PC * PC
    diagonal = (iota((size, 128), 0) == iota((size, 128), 1)) & (iota((size, 128), 0) < params)
    blocks = [mat[c, t, :size, :] + jnp.where(diagonal, ridge, 0.0) for c in chains]
    for c, inverse in zip(chains, inverted(blocks, params)):
        right = side[c, t]
        w = dot(inverse, right, (1, 0))
        solved[c, t] = w
        schur = dot(right[:size, :256], w, (0, 0))
        mat[c, t + 1] -= schur[:128, :128]
        side[c, t + 1, :, 0:128] -= schur[:128, 128:256]
        side[c, t + 1, :, 256:384] -= schur[:128, 256:384]
        mat[c, t + 2] -= schur[128:, 128:256]
        side[c, t + 2, :, 256:384] -= schur[128:, 256:384]


def solve_zone(fields, mat, side, solved, answer):
    size = fields.shape[1]
    squares = jnp.zeros((size, 128), F32)
    for number in range(3 * FIELDS):
        if number % FIELDS < FIELDS - 1:
            squares = squares + fields[number] * fields[number]
    trace = jnp.sum(jnp.sum(squares, axis=0, keepdims=True), axis=1, keepdims=True)
    ridge = DAMPING * trace / PC**3 + EPSILON
    meet = PC // 2 - 1

    def both(t, _):
        eliminate(t, (0, 1), size, ridge, mat, side, solved)
        return 0

    lax.fori_loop(0, meet, both, 0)
    mat[0, meet] += mat[1, meet + 1]
    mat[0, meet + 1] += mat[1, meet]
    side[0, meet, :, 0:128] += side[1, meet, :, 0:128].T
    side[0, meet, :, 256:384] += side[1, meet + 1, :, 256:384]
    side[0, meet + 1, :, 256:384] += side[1, meet, :, 256:384]

    def single(t, _):
        eliminate(t, (0,), size, ridge, mat, side, solved)
        return 0

    lax.fori_loop(meet, meet + 2, single, 0)
    answer[...] = jnp.zeros_like(answer)

    def back(t, c):
        value = solved[c, t, :, 256:384]
        value = value - dot(solved[c, t, :, 0:128], answer[c, t + 1], (1, 0))
        value = value - dot(solved[c, t, :, 128:256], answer[c, t + 2], (1, 0))
        answer[c, t, :size, :] = value

    answer[0, meet + 1, :size, :] = solved[0, meet + 1, :, 256:384]
    value = solved[0, meet, :, 256:384]
    answer[0, meet, :size, :] = value - dot(solved[0, meet, :, 0:128], answer[0, meet + 1], (1, 0))
    answer[1, meet] = answer[0, meet + 1]
    answer[1, meet + 1] = answer[0, meet]
    for t in range(meet - 1, -1, -1):
        for c in range(2):
            back(t, c)


def place_zone(begin, zone_m, answer, spread, temp, added):
    rows = zone_m.shape[1]
    span = 2 * PC
    lane = iota((128, 128), 1)
    update = jnp.zeros((128, 128), F32)
    for z in range(PC):
        value = answer[0, z] if z < PC // 2 else answer[1, PC - 1 - z]
        update = jnp.where((lane == 2 * z + 1) | (lane == 2 * z + 2), -value, update)
    spread[...] = update

    def ramp(position):
        value = jnp.sin(math.pi * (position.astype(F32) - 0.5) / span)
        return jnp.where((position >= 1) & (position <= span), value, 0.0)

    weight = ramp(iota((rows, 128), 0)) * ramp(iota((rows, 128), 1))
    temp[0] = jnp.zeros_like(weight)
    for x in range(PC):
        part = spread[x * PC : (x + 1) * PC, :]
        temp[0, pl.ds(1, PC, stride=2), :] = part
        temp[0, pl.ds(2, PC, stride=2), :] = part
        value = weight * temp[0]
        for a in range(2):
            at = 2 * x + 1 + a
            plane = value * math.sin(math.pi * (at - 0.5) / span) * zone_m[at]
            plane = jnp.pad(plane, ((0, added.shape[1] - rows), (0, 0)))
            plane = pltpu.roll(plane, begin[1] - FSWEEPS, 0)
            plane = jnp.pad(plane, ((0, 0), (0, added.shape[2] - 128)))
            plane = pltpu.roll(plane, begin[2] - FSWEEPS, 1)
            added[begin[0] - FSWEEPS + at] += plane


def pack_kernel(margin, across, low_out, high_out):
    channels, span_x, rows, lanes = across.shape
    room = 128 // margin
    lane = iota((rows, 128), 1)

    def pack(k, _):
        for group in range(low_out.shape[1]):
            low = high = jnp.zeros((rows, 128), F32)
            for j in range(min(room, span_x - group * room)):
                x = group * room + j
                here = (lane >= j * margin) & (lane < (j + 1) * margin)
                low = jnp.where(here, roll(across[k, x, :, :128], j * margin, 1), low)
                last = across[k, x, :, lanes - 128 :]
                high = jnp.where(here, roll(last, j * margin + margin, 1), high)
            low_out[k, group] = low
            high_out[k, group] = high
        return 0

    lax.fori_loop(0, channels, pack, 0)


def widen(margin, across, from_low, from_high, wide):
    channels, span_x, rows, lanes = across.shape
    room = 128 // margin
    lane = iota((rows, 128), 1)

    def spread(k, _):
        for x in range(span_x):
            group, j = x // room, x % room
            high = roll(from_high[k, group], -j * margin, 1)
            low = roll(from_low[k, group], -j * margin - margin, 1)
            halo = jnp.where(lane < margin, high, jnp.where(lane >= 128 - margin, low, 0.0))
            wide[k, x, :, :lanes] = across[k, x]
            wide[k, x, :, lanes:] = halo
        return 0

    lax.fori_loop(0, channels, spread, 0)


def kernel(totals, brick, margin, starts, across, from_low, from_high, field_out, added, wide, *scratch):
    widen(margin, across, from_low, from_high, wide)
    (buf_a, buf_b, mx, my, mz, inverse, zone_u, zone_f, zone_m) = scratch[:9]
    temp, fields, strip, mat, side, solved, answer, spread = scratch[9:]
    source = relax_planes(
        totals, brick, margin, wide, field_out, (buf_a, buf_b), (mx, my, mz, inverse)
    )
    added[...] = jnp.zeros_like(added)
    for number in range(starts.shape[0]):
        begin = [starts[number, axis] for axis in range(3)]
        cut_zone(begin, margin, source, wide, zone_u, zone_f, zone_m)
        fields[...] = jnp.zeros_like(fields)
        coarse_fields(zone_u, zone_f, zone_m, temp, fields)
        assemble(fields, strip, mat, side)
        solve_zone(fields, mat, side, solved, answer)
        place_zone(begin, zone_m, answer, spread, temp, added)


def exchange(first, last, axis):
    count = lax.axis_size(axis)
    forward = [(i, i + 1) for i in range(count - 1)]
    backward = [(target, source) for source, target in forward]
    return lax.ppermute(last, axis, forward), lax.ppermute(first, axis, backward)


def body(forcing, start_field, modulus, corners):
    brick = modulus.shape
    lower = [lax.axis_index(n) * size for n, size in zip(("gx", "gy", "gz"), brick)]
    totals = [lax.axis_size(n) * size for n, size in zip(("gx", "gy", "gz"), brick)]
    margin = HALO + FSWEEPS
    stacked = jnp.concatenate([start_field, forcing, modulus[None]], axis=0)
    channels = stacked.shape[0]
    x_low, x_high = exchange(stacked[:, :margin], stacked[:, -margin:], "gx")
    y_low, y_high = exchange(stacked[:, :, :margin], stacked[:, :, -margin:], "gy")
    sides = jnp.stack([y_low, y_high])
    low_ends, high_ends = exchange(sides[:, :, :margin], sides[:, :, -margin:], "gx")
    across = jnp.concatenate(
        [
            jnp.concatenate([low_ends[0], x_low, low_ends[1]], axis=2),
            jnp.concatenate([y_low, stacked, y_high], axis=2),
            jnp.concatenate([high_ends[0], x_high, high_ends[1]], axis=2),
        ],
        axis=1,
    )
    span_x, span_y = across.shape[1:3]
    rows, lanes = -(-span_y // 8) * 8, brick[2] + 128
    across = jnp.pad(across, ((0, 0), (0, 0), (0, rows - span_y), (0, 0)))
    groups = -(-span_x // (128 // margin))
    packed = jax.ShapeDtypeStruct((channels, groups, rows, 128), F32)
    whole = pl.BlockSpec(memory_space=pltpu.VMEM)
    limit = pltpu.CompilerParams(vmem_limit_bytes=56 * 1024 * 1024)
    z_low, z_high = pl.pallas_call(
        functools.partial(pack_kernel, margin),
        out_shape=(packed, packed),
        in_specs=[whole],
        out_specs=(whole, whole),
        compiler_params=limit,
    )(across)
    z_low, z_high = exchange(z_low, z_high, "gz")
    starts = (corners - jnp.stack(lower).astype(jnp.int32)[None, :] + margin - 1).astype(jnp.int32)
    zone_span = 2 * PC + 2
    zone_rows = -(-zone_span // 8) * 8
    size = -(-PC * PC // 8) * 8
    planes = PC // 2 + 3
    plane_buffer = pltpu.VMEM((span_x, rows, lanes), F32)
    reach = tuple(size + 2 * HALO for size in brick)
    field, added = pl.pallas_call(
        functools.partial(kernel, totals, brick, margin),
        out_shape=(
            jax.ShapeDtypeStruct(forcing.shape, F32),
            jax.ShapeDtypeStruct((reach[0], rows, lanes), F32),
        ),
        in_specs=[pl.BlockSpec(memory_space=pltpu.SMEM), whole, whole, whole],
        out_specs=(whole, whole),
        scratch_shapes=[
            pltpu.VMEM((channels, span_x, rows, lanes), F32),
            pltpu.VMEM((3, span_x, rows, lanes), F32),
            pltpu.VMEM((3, span_x, rows, lanes), F32),
            plane_buffer, plane_buffer, plane_buffer, plane_buffer,
            pltpu.VMEM((3, zone_span, zone_rows, 128), F32),
            pltpu.VMEM((3, zone_span, zone_rows, 128), F32),
            pltpu.VMEM((zone_span, zone_rows, 128), F32),
            pltpu.VMEM((3 * FIELDS, zone_rows, 128), F32),
            pltpu.VMEM((3 * FIELDS, size, 128), F32),
            pltpu.VMEM((3 * size, 512), F32),
            pltpu.VMEM((2, planes, 128, 128), F32),
            pltpu.VMEM((2, planes, 128, 384), F32),
            pltpu.VMEM((2, planes, size, 384), F32),
            pltpu.VMEM((2, planes, 128, 128), F32),
            pltpu.VMEM((128, 128), F32),
        ],
        compiler_params=limit,
    )(starts, across, z_low, z_high)
    summed = added[:, : reach[1], : reach[2]]
    received = extended(pack_margins(summed, 0, HALO), (("gx", 0),), HALO)
    summed = fold_margins(summed, received, 0, HALO)
    received = extended(pack_margins(summed, 1, HALO), (("gy", 1),), HALO)
    summed = fold_margins(summed, received, 1, HALO)
    received = extended(pack_margins(summed, 2, HALO), (("gz", 2),), HALO)
    summed = fold_margins(summed, received, 2, HALO)
    return (field, modulus + summed)


def solution(mesh):
    placed = (
        P(None, "gx", "gy", "gz"),
        P(None, "gx", "gy", "gz"),
        P("gx", "gy", "gz"),
        P(("gx", "gy", "gz"), None),
    )
    return jax.shard_map(
        body,
        mesh=mesh,
        in_specs=placed,
        out_specs=(P(None, "gx", "gy", "gz"), P("gx", "gy", "gz")),
        check_vma=False,
    )
```

profile of v0, /device:TPU:0, one launch (start us, length us, event | category | flops | bytes accessed | tf_op | source)
XLA Modules:
  0.0 216.1 jit_solution(10976519619328197471)
XLA Ops:
  0.6 1.2 pad_maximum_fusion.1
  1.9 0.2 fusion.12
  2.0 0.2 copy.6
  2.2 4.9 %collective-permute-start = (f32[7,16,10,128]{3,1,2,0:T(8,128)S(1)}, f32[7,16,10,128]{3,1,2,0:T(8,128)S(1)}, u32[]{:S(2)}, u32[]{:S(2)}) collective-permute-start(f32[7,16,10,128]{3,1,2,0:T(8,128)S(1)} %copy.6), channel_id=1, source_target_pairs={{0,2},{2,4},{4,6},{1,3},{3,5},{5,7},{8,10},{10,12},{12,14},{9,11},... | collective-permute-start | bytes 1720328 | tf_op jit(solution)/shard_map/ppermute | solution.py:420
  7.1 0.2 copy.7
  7.3 1.3 collective-permute-start.1
  8.6 10.7 %collective-permute-done = f32[7,16,10,128]{3,1,2,0:T(8,128)S(1)} collective-permute-done((f32[7,16,10,128]{3,1,2,0:T(8,128)S(1)}, f32[7,16,10,128]{3,1,2,0:T(8,128)S(1)}, u32[]{:S(2)}, u32[]{:S(2)}) %collective-permute-start) | collective-permute-done | bytes 573472 | tf_op jit(solution)/shard_map/ppermute | solution.py:420
  19.3 14.2 %collective-permute-done.1 = f32[7,16,10,128]{3,1,2,0:T(8,128)S(1)} collective-permute-done((f32[7,16,10,128]{3,1,2,0:T(8,128)S(1)}, f32[7,16,10,128]{3,1,2,0:T(8,128)S(1)}, u32[]{:S(2)}, u32[]{:S(2)}) %collective-permute-start.1) | collective-permute-done | bytes 573472 | tf_op jit(solution)/shard_map/ppermute | solution.py:420
  33.5 0.2 slice_maximum_fusion
  33.8 0.6 copy.8
  34.3 3.5 %collective-permute-start.2 = (f32[2,7,10,10,128]{4,0,3,2,1:T(2,128)S(1)}, f32[2,7,10,10,128]{4,0,3,2,1:T(2,128)S(1)}, u32[]{:S(2)}, u32[]{:S(2)}) collective-permute-start(f32[2,7,10,10,128]{4,0,3,2,1:T(2,128)S(1)} %copy.8), channel_id=1, source_target_pairs={{0,8},{8,16},{16,24},{1,9},{9,17},{17,25},{2,10},{10,18},{18,26},{... | collective-permute-start | bytes 2150408 | tf_op jit(solution)/shard_map/ppermute | solution.py:420
  37.9 0.6 copy.13
  38.4 1.3 collective-permute-start.4
  39.7 0.1 fusion.11
  39.9 0.0 copy-start
  39.9 0.0 copy-start.1
  39.9 0.0 copy-start.2
  39.9 4.7 %collective-permute-start.3 = (f32[7,10,16,128]{3,2,1,0:T(8,128)S(1)}, f32[7,10,16,128]{3,2,1,0:T(8,128)S(1)}, u32[]{:S(2)}, u32[]{:S(2)}) collective-permute-start(f32[7,10,16,128]{3,2,1,0:T(8,128)S(1)} %get-tuple-element.14), channel_id=1, source_target_pairs={{0,8},{8,16},{16,24},{1,9},{9,17},{17,25},{2,10},{10,18},{18,26},{... | collective-permute-start | bytes 1720328 | tf_op jit(solution)/shard_map/ppermute | solution.py:420
  44.6 1.3 collective-permute-start.5
  45.9 0.2 copy.11
  46.1 0.2 copy.12
  46.3 8.0 %collective-permute-done.2 = f32[2,7,10,10,128]{4,0,3,2,1:T(2,128)S(1)} collective-permute-done((f32[2,7,10,10,128]{4,0,3,2,1:T(2,128)S(1)}, f32[2,7,10,10,128]{4,0,3,2,1:T(2,128)S(1)}, u32[]{:S(2)}, u32[]{:S(2)}) %collective-permute-start.2) | collective-permute-done | bytes 716832 | tf_op jit(solution)/shard_map/ppermute | solution.py:420
  54.3 0.6 fusion.13
  54.9 4.4 %collective-permute-done.4 = f32[2,7,10,10,128]{4,0,3,2,1:T(2,128)S(1)} collective-permute-done((f32[2,7,10,10,128]{4,0,3,2,1:T(2,128)S(1)}, f32[2,7,10,10,128]{4,0,3,2,1:T(2,128)S(1)}, u32[]{:S(2)}, u32[]{:S(2)}) %collective-permute-start.4) | collective-permute-done | bytes 716832 | tf_op jit(solution)/shard_map/ppermute | solution.py:420
  59.3 0.6 fusion.14
  59.9 0.1 copy_bitcast_fusion.2
  60.0 0.1 copy_bitcast_fusion
  60.1 4.4 %collective-permute-done.3 = f32[7,10,16,128]{3,2,1,0:T(8,128)S(1)} collective-permute-done((f32[7,10,16,128]{3,2,1,0:T(8,128)S(1)}, f32[7,10,16,128]{3,2,1,0:T(8,128)S(1)}, u32[]{:S(2)}, u32[]{:S(2)}) %collective-permute-start.3) | collective-permute-done | bytes 573472 | tf_op jit(solution)/shard_map/ppermute | solution.py:420
  64.5 4.7 %collective-permute-done.5 = f32[7,10,16,128]{3,2,1,0:T(8,128)S(1)} collective-permute-done((f32[7,10,16,128]{3,2,1,0:T(8,128)S(1)}, f32[7,10,16,128]{3,2,1,0:T(8,128)S(1)}, u32[]{:S(2)}, u32[]{:S(2)}) %collective-permute-start.5) | collective-permute-done | bytes 573472 | tf_op jit(solution)/shard_map/ppermute | solution.py:420
  69.3 0.0 copy-done
  69.3 0.0 copy-done.1
  69.3 0.0 copy-done.2
  69.3 7.5 %fusion.across = f32[7,36,40,128]{3,2,1,0:T(8,128)} fusion(f32[7,10,10,128]{3,2,1,0:T(8,128)S(1)} %get-tuple-element.26, f32[7,10,16,128]{3,2,1,0:T(8,128)S(1)} %collective-permute-done.5, f32[7,10,10,128]{3,2,1,0:T(8,128)S(1)} %get-tuple-element.27, f32[7,16,10,128]{3,2,1,0:T(8,128)S(1)} %copy.12, f32[7,10,10,128]{3,2,1,0:T(8,128)S(1)} %get-tuple-element.28, ...), kind=kLoop, calls=%fused_computation.1 | loop fusion | flops 28385280 | bytes 9805824 | tf_op jit(solution)/shard_map/concatenate | solution.py:434
  76.8 0.0 copy-start.5
  76.8 6.4 %shard_map.59 = (f32[7,3,40,128]{3,2,1,0:T(8,128)}, f32[7,3,40,128]{3,2,1,0:T(8,128)}) custom-call(f32[7,36,40,128]{3,2,1,0:T(8,128)} %fusion.across), custom_call_target="tpu_custom_call" | custom-call | tf_op jit(solution)/shard_map/pallas_call | solution.py:449
  83.2 1.3 collective-permute-start.6
  84.5 1.3 collective-permute-start.7
  85.9 0.0 copy-done.5
  85.9 0.7 fusion.9.starts
  86.5 0.0 collective-permute-done.6.from_low
  86.5 0.0 copy-start.3
  86.5 1.9 collective-permute-done.7.from_high
  88.4 0.0 copy-done.3
  88.4 0.8 copy-done.4
  89.2 96.8 %shard_map.60 = (f32[3,16,16,128]{3,2,1,0:T(8,128)}, f32[28,40,256]{2,1,0:T(8,128)}) custom-call(s32[1,3]{1,0:T(1,128)} %fusion.9.starts, f32[7,36,40,128]{3,2,1,0:T(8,128)} %fusion.across, f32[7,3,40,128]{3,2,1,0:T(8,128)} %copy-done.3, f32[7,3,40,128]{3,2,1,0:T(8,128)} %copy-done.4), custom_call_target="tpu_custom_call" | custom-call | tf_op jit(solution)/shard_map/pallas_call | solution.py:464
  186.0 1.0 fusion.10
  187.1 3.5 %collective-permute-start.8 = (f32[6,28,140]{2,1,0:T(8,128)S(1)}, f32[6,28,140]{2,1,0:T(8,128)S(1)}, u32[]{:S(2)}, u32[]{:S(2)}) collective-permute-start(f32[6,28,140]{2,1,0:T(8,128)S(1)} %get-tuple-element.10), channel_id=1, source_target_pairs={{0,8},{8,16},{16,24},{1,9},{9,17},{17,25},{2,10},{10,18},{18,26},{... | collective-permute-start | bytes 282248 | tf_op jit(solution)/shard_map/ppermute | solution.py:29
  190.5 1.3 collective-permute-start.9
  191.9 0.1 pad.12.clone
  191.9 3.0 %collective-permute-done.8 = f32[6,28,140]{2,1,0:T(8,128)S(1)} collective-permute-done((f32[6,28,140]{2,1,0:T(8,128)S(1)}, f32[6,28,140]{2,1,0:T(8,128)S(1)}, u32[]{:S(2)}, u32[]{:S(2)}) %collective-permute-start.8) | collective-permute-done | bytes 94112 | tf_op jit(solution)/shard_map/ppermute | solution.py:29
  195.0 4.1 %collective-permute-done.9 = f32[6,28,140]{2,1,0:T(8,128)S(1)} collective-permute-done((f32[6,28,140]{2,1,0:T(8,128)S(1)}, f32[6,28,140]{2,1,0:T(8,128)S(1)}, u32[]{:S(2)}, u32[]{:S(2)}) %collective-permute-start.9) | collective-permute-done | bytes 94112 | tf_op jit(solution)/shard_map/ppermute | solution.py:32
  199.1 1.2 maximum_add_fusion
  200.3 3.4 %collective-permute-start.10 = (f32[16,6,140]{2,1,0:T(8,128)S(1)}, f32[16,6,140]{2,1,0:T(8,128)S(1)}, u32[]{:S(2)}, u32[]{:S(2)}) collective-permute-start(f32[16,6,140]{2,1,0:T(8,128)S(1)} %get-tuple-element.22), channel_id=1, source_target_pairs={{0,2},{2,4},{4,6},{1,3},{3,5},{5,7},{8,10},{10,12},{12,14},{9,11},... | collective-permute-start | bytes 161288 | tf_op jit(solution)/shard_map/ppermute | solution.py:29
  203.7 1.3 collective-permute-start.11
  205.0 1.2 collective-permute-done.10
  206.2 4.4 %collective-permute-done.11 = f32[16,6,140]{2,1,0:T(8,128)S(1)} collective-permute-done((f32[16,6,140]{2,1,0:T(8,128)S(1)}, f32[16,6,140]{2,1,0:T(8,128)S(1)}, u32[]{:S(2)}, u32[]{:S(2)}) %collective-permute-start.11) | collective-permute-done | bytes 53792 | tf_op jit(solution)/shard_map/ppermute | solution.py:32
  210.6 0.1 slice_add_fusion
  210.7 0.1 fusion.16
  210.8 1.3 collective-permute-start.12
  212.1 1.3 collective-permute-start.13
  213.4 0.1 pad.6.clone
  213.5 0.0 collective-permute-done.12
  213.5 1.9 collective-permute-done.13
  215.3 0.8 fusion.7
  (4 shorter events, 0.0 us)
Async XLA Ops:
  2.2 17.1 %collective-permute-start = (f32[7,16,10,128]{3,1,2,0:T(8,128)S(1)}, f32[7,16,10,128]{3,1,2,0:T(8,128)S(1)}, u32[]{:S(2)}, u32[]{:S(2)}) collective-permute-start(f32[7,16,10,128]{3,1,2,0:T(8,128)S(1)} %copy.6), channel_id=1, source_target_pairs={{0,2},{2,4},{4,6},{1,3},{3,5},{5,7},{8,10},{10,12},{12,14},{9,11},... | collective-permute-start | bytes 1720328 | tf_op jit(solution)/shard_map/ppermute | solution.py:420
  7.3 26.2 %collective-permute-start.1 = (f32[7,16,10,128]{3,1,2,0:T(8,128)S(1)}, f32[7,16,10,128]{3,1,2,0:T(8,128)S(1)}, u32[]{:S(2)}, u32[]{:S(2)}) collective-permute-start(f32[7,16,10,128]{3,1,2,0:T(8,128)S(1)} %copy.7), channel_id=1, source_target_pairs={{2,0},{4,2},{6,4},{3,1},{5,3},{7,5},{10,8},{12,10},{14,12},{11,9},... | collective-permute-start | bytes 1720328 | tf_op jit(solution)/shard_map/ppermute | solution.py:420
  34.3 20.0 %collective-permute-start.2 = (f32[2,7,10,10,128]{4,0,3,2,1:T(2,128)S(1)}, f32[2,7,10,10,128]{4,0,3,2,1:T(2,128)S(1)}, u32[]{:S(2)}, u32[]{:S(2)}) collective-permute-start(f32[2,7,10,10,128]{4,0,3,2,1:T(2,128)S(1)} %copy.8), channel_id=1, source_target_pairs={{0,8},{8,16},{16,24},{1,9},{9,17},{17,25},{2,10},{10,18},{18,26},{... | collective-permute-start | bytes 2150408 | tf_op jit(solution)/shard_map/ppermute | solution.py:420
  38.4 20.9 %collective-permute-start.4 = (f32[2,7,10,10,128]{4,0,3,2,1:T(2,128)S(1)}, f32[2,7,10,10,128]{4,0,3,2,1:T(2,128)S(1)}, u32[]{:S(2)}, u32[]{:S(2)}) collective-permute-start(f32[2,7,10,10,128]{4,0,3,2,1:T(2,128)S(1)} %copy.13), channel_id=1, source_target_pairs={{8,0},{16,8},{24,16},{9,1},{17,9},{25,17},{10,2},{18,10},{26,18},{... | collective-permute-start | bytes 2150408 | tf_op jit(solution)/shard_map/ppermute | solution.py:420
  39.9 29.4 %copy-start = (f32[3,16,16,128]{3,2,1,0:T(8,128)S(1)}, f32[3,16,16,128]{3,2,1,0:T(8,128)}, u32[]{:S(2)}) copy-start(f32[3,16,16,128]{3,2,1,0:T(8,128)} %param.4) | copy-start | bytes 1179652
  39.9 29.4 %copy-start.1 = (f32[3,16,16,128]{3,2,1,0:T(8,128)S(1)}, f32[3,16,16,128]{3,2,1,0:T(8,128)}, u32[]{:S(2)}) copy-start(f32[3,16,16,128]{3,2,1,0:T(8,128)} %param.5) | copy-start | bytes 1179652
  39.9 29.4 %copy-start.2 = (f32[16,16,128]{2,1,0:T(8,128)S(1)}, f32[16,16,128]{2,1,0:T(8,128)}, u32[]{:S(2)}) copy-start(f32[16,16,128]{2,1,0:T(8,128)} %param.6) | copy-start | bytes 393220
  39.9 24.6 %collective-permute-start.3 = (f32[7,10,16,128]{3,2,1,0:T(8,128)S(1)}, f32[7,10,16,128]{3,2,1,0:T(8,128)S(1)}, u32[]{:S(2)}, u32[]{:S(2)}) collective-permute-start(f32[7,10,16,128]{3,2,1,0:T(8,128)S(1)} %get-tuple-element.14), channel_id=1, source_target_pairs={{0,8},{8,16},{16,24},{1,9},{9,17},{17,25},{2,10},{10,18},{18,26},{... | collective-permute-start | bytes 1720328 | tf_op jit(solution)/shard_map/ppermute | solution.py:420
  44.6 24.6 %collective-permute-start.5 = (f32[7,10,16,128]{3,2,1,0:T(8,128)S(1)}, f32[7,10,16,128]{3,2,1,0:T(8,128)S(1)}, u32[]{:S(2)}, u32[]{:S(2)}) collective-permute-start(f32[7,10,16,128]{3,2,1,0:T(8,128)S(1)} %get-tuple-element.15), channel_id=1, source_target_pairs={{8,0},{16,8},{24,16},{9,1},{17,9},{25,17},{10,2},{18,10},{26,18},{... | collective-permute-start | bytes 1720328 | tf_op jit(solution)/shard_map/ppermute | solution.py:420
  76.8 9.1 %copy-start.5 = (s32[1,3]{1,0:T(1,128)S(1)}, s32[1,3]{1,0:T(1,128)}, u32[]{:S(2)}) copy-start(s32[1,3]{1,0:T(1,128)} %param.7) | copy-start | bytes 40
  83.2 3.3 %collective-permute-start.6 = (f32[7,3,40,128]{3,2,1,0:T(8,128)}, f32[7,3,40,128]{3,2,1,0:T(8,128)S(1)}, u32[]{:S(2)}, u32[]{:S(2)}) collective-permute-start(f32[7,3,40,128]{3,2,1,0:T(8,128)} %get-tuple-element.6), channel_id=1, source_target_pairs={{0,1},{2,3},{4,5},{6,7},{8,9},{10,11},{12,13},{14,15},{16,17},{18,... | collective-permute-start | bytes 1290248 | tf_op jit(solution)/shard_map/ppermute | solution.py:420
  84.5 3.9 %collective-permute-start.7 = (f32[7,3,40,128]{3,2,1,0:T(8,128)}, f32[7,3,40,128]{3,2,1,0:T(8,128)S(1)}, u32[]{:S(2)}, u32[]{:S(2)}) collective-permute-start(f32[7,3,40,128]{3,2,1,0:T(8,128)} %get-tuple-element.7), channel_id=1, source_target_pairs={{1,0},{3,2},{5,4},{7,6},{9,8},{11,10},{13,12},{15,14},{17,16},{19,... | collective-permute-start | bytes 1290248 | tf_op jit(solution)/shard_map/ppermute | solution.py:420
  86.5 1.9 copy-start.3
  88.4 0.8 copy-start.4
  187.1 7.9 %collective-permute-start.8 = (f32[6,28,140]{2,1,0:T(8,128)S(1)}, f32[6,28,140]{2,1,0:T(8,128)S(1)}, u32[]{:S(2)}, u32[]{:S(2)}) collective-permute-start(f32[6,28,140]{2,1,0:T(8,128)S(1)} %get-tuple-element.10), channel_id=1, source_target_pairs={{0,8},{8,16},{16,24},{1,9},{9,17},{17,25},{2,10},{10,18},{18,26},{... | collective-permute-start | bytes 282248 | tf_op jit(solution)/shard_map/ppermute | solution.py:29
  190.5 8.6 %collective-permute-start.9 = (f32[6,28,140]{2,1,0:T(8,128)S(1)}, f32[6,28,140]{2,1,0:T(8,128)S(1)}, u32[]{:S(2)}, u32[]{:S(2)}) collective-permute-start(f32[6,28,140]{2,1,0:T(8,128)S(1)} %get-tuple-element.11), channel_id=1, source_target_pairs={{8,0},{16,8},{24,16},{9,1},{17,9},{25,17},{10,2},{18,10},{26,18},{... | collective-permute-start | bytes 282248 | tf_op jit(solution)/shard_map/ppermute | solution.py:32
  200.3 5.9 %collective-permute-start.10 = (f32[16,6,140]{2,1,0:T(8,128)S(1)}, f32[16,6,140]{2,1,0:T(8,128)S(1)}, u32[]{:S(2)}, u32[]{:S(2)}) collective-permute-start(f32[16,6,140]{2,1,0:T(8,128)S(1)} %get-tuple-element.22), channel_id=1, source_target_pairs={{0,2},{2,4},{4,6},{1,3},{3,5},{5,7},{8,10},{10,12},{12,14},{9,11},... | collective-permute-start | bytes 161288 | tf_op jit(solution)/shard_map/ppermute | solution.py:29
  203.7 6.9 %collective-permute-start.11 = (f32[16,6,140]{2,1,0:T(8,128)S(1)}, f32[16,6,140]{2,1,0:T(8,128)S(1)}, u32[]{:S(2)}, u32[]{:S(2)}) collective-permute-start(f32[16,6,140]{2,1,0:T(8,128)S(1)} %get-tuple-element.23), channel_id=1, source_target_pairs={{2,0},{4,2},{6,4},{3,1},{5,3},{7,5},{10,8},{12,10},{14,12},{11,9},... | collective-permute-start | bytes 161288 | tf_op jit(solution)/shard_map/ppermute | solution.py:32
  210.8 2.7 %collective-permute-start.12 = (f32[16,16,6]{2,1,0:T(8,128)S(1)}, f32[16,16,6]{2,1,0:T(8,128)S(1)}, u32[]{:S(2)}, u32[]{:S(2)}) collective-permute-start(f32[16,16,6]{2,1,0:T(8,128)S(1)} %get-tuple-element.24), channel_id=1, source_target_pairs={{0,1},{2,3},{4,5},{6,7},{8,9},{10,11},{12,13},{14,15},{16,17},{18,... | collective-permute-start | bytes 18440 | tf_op jit(solution)/shard_map/ppermute | solution.py:29
  212.1 3.2 %collective-permute-start.13 = (f32[16,16,6]{2,1,0:T(8,128)S(1)}, f32[16,16,6]{2,1,0:T(8,128)S(1)}, u32[]{:S(2)}, u32[]{:S(2)}) collective-permute-start(f32[16,16,6]{2,1,0:T(8,128)S(1)} %get-tuple-element.25), channel_id=1, source_target_pairs={{1,0},{3,2},{5,4},{7,6},{9,8},{11,10},{13,12},{15,14},{17,16},{19,... | collective-permute-start | bytes 18440 | tf_op jit(solution)/shard_map/ppermute | solution.py:32
where the time goes:
time: 217 us; the launch traced here: 216 us
  Pallas kernels  103 us (47%)
  waiting for transfers between devices  63 us (29%)
  starting transfers between devices  31.6 us (15%)
  other arithmetic  11.7 us (5%)
  local copies, waits for them, and re-layouts  5.57 us (3%)
    pallas_call x1, Pallas kernels, body(): pl.pallas_call(functools.partial(kernel, totals, brick, margin), out_shap...  96.8 us
    ppermute x4, waiting for transfers between devices, exchange(): lax.ppermute(first, axis, backward)  25.3 us
    ppermute x4, waiting for transfers between devices, exchange(): lax.ppermute(last, axis, forward)  23.1 us
    ppermute x4, starting transfers between devices, exchange(): lax.ppermute(last, axis, forward)  14.4 us
    ppermute x3, waiting for transfers between devices, extended(): lax.ppermute(lax.slice_in_dim(block, 0, width, axis=dim), axis, backward)  10.3 us
    ppermute x3, starting transfers between devices, extended(): lax.ppermute(lax.slice_in_dim(block, block.shape[dim] - width, None, axis...  8.16 us
    concatenate x1, other arithmetic, body(): jnp.concatenate([jnp.concatenate([low_ends[0], x_low, low_ends[1]], axis=...  7.53 us
    pallas_call x1, Pallas kernels, body(): pl.pallas_call(functools.partial(pack_kernel, margin), out_shape=(packed,...  6.43 us
  transfers between devices with their start and end apart: 14, of which 12 were waited for; matrix products, arithmetic and copies ran while one was open for 2% of the time, Pallas kernels for 0%

commit v1 on v0

v1 whole, which is shorter than its diff:
```python
import functools
import math

import jax
import jax.numpy as jnp
from jax import lax
from jax.experimental import pallas as pl
from jax.experimental.pallas import tpu as pltpu
from jax.sharding import PartitionSpec as P

PC = 10
HALO = 6
FSWEEPS = 4


MASS_TERM = 0.5
DAMPING = 0.1
EPSILON = 1e-06
HIGHEST = lax.Precision.HIGHEST
PANEL = 2
F32 = jnp.float32


def dot(a, b, contract):
    return lax.dot_general(
        a, b, ((contract[:1], contract[1:]), ((), ())), precision=HIGHEST, preferred_element_type=F32
    )


def roll(values, shift, axis):
    return pltpu.roll(values, shift % values.shape[axis], axis)


def iota(shape, axis):
    return lax.broadcasted_iota(jnp.int32, shape, axis)


MESH_ID = pl.DeviceIdType.MESH
AXES = ("gx", "gy", "gz")
AROUND = tuple((dx, dy) for dx in (-1, 0, 1) for dy in (-1, 0, 1) if (dx, dy) != (0, 0))
FACES = ((-1, 0, 0), (1, 0, 0), (0, -1, 0), (0, 1, 0), (0, 0, -1), (0, 0, 1))


class Place:
    def __init__(self, counts):
        self.counts = counts
        self.here = [lax.axis_index(name) for name in AXES]

    def exists(self, step):
        inside = None
        for at, count, move in zip(self.here, self.counts, step):
            if move:
                test = at + move < count if move > 0 else at + move >= 0
                inside = test if inside is None else inside & test
        return inside

    def device(self, step):
        return tuple(at + move for at, move in zip(self.here, step))

    def peer(self, turn):
        return self.here[:2] + [lax.rem(self.here[2] + turn, self.counts[2])]

    def greet(self):
        barrier = pltpu.get_barrier_semaphore()
        total = self.counts[2] - 1
        for dx, dy in AROUND:
            step = (dx, dy, 0)

            @pl.when(self.exists(step))
            def _():
                pl.semaphore_signal(
                    barrier, inc=1, device_id=self.device(step), device_id_type=MESH_ID
                )

            total = total + self.exists(step).astype(jnp.int32)
        for turn in range(1, self.counts[2]):
            pl.semaphore_signal(
                barrier, inc=1, device_id=tuple(self.peer(turn)), device_id_type=MESH_ID
            )
        pl.semaphore_wait(barrier, total)


def opposite(step):
    return tuple(-move for move in step)


class Message:
    def __init__(self, place, step, source, target, send, recv):
        self.place, self.step = place, step
        self.copy = pltpu.make_async_remote_copy(
            src_ref=source,
            dst_ref=target,
            send_sem=send,
            recv_sem=recv,
            device_id=place.device(step),
            device_id_type=MESH_ID,
        )

    def start(self):
        pl.when(self.place.exists(self.step))(self.copy.start)

    def sent(self):
        pl.when(self.place.exists(self.step))(self.copy.wait_send)

    def arrived(self):
        pl.when(self.place.exists(opposite(self.step)))(self.copy.wait_recv)


def edge_span(move, size, margin):
    if move > 0:
        return slice(size, size + margin), slice(0, margin)
    if move < 0:
        return slice(margin, 2 * margin), slice(margin + size, 2 * margin + size)
    return slice(margin, margin + size), slice(margin, margin + size)


def spread_messages(place, brick, margins, ref, lanes, send, recv):
    messages = []
    for n, (dx, dy) in enumerate(AROUND):
        from_x, to_x = edge_span(dx, brick[0], margins[0])
        from_y, to_y = edge_span(dy, brick[1], margins[1])
        messages.append(
            Message(
                place,
                (dx, dy, 0),
                ref.at[:, from_x, from_y, lanes],
                ref.at[:, to_x, to_y, lanes],
                send.at[n],
                recv.at[n],
            )
        )
    return messages


def peer_copies(place, ref, lanes, send, recv):
    return [
        pltpu.make_async_remote_copy(
            src_ref=ref.at[:, :, :, lanes],
            dst_ref=ref.at[:, :, :, lanes],
            send_sem=send.at[turn - 1],
            recv_sem=recv.at[turn - 1],
            device_id=tuple(place.peer(turn)),
            device_id_type=MESH_ID,
        )
        for turn in range(1, place.counts[2])
    ]


def clear_outside(place, brick, margins, refs, lanes):
    for dx, dy in AROUND:
        _, to_x = edge_span(-dx, brick[0], margins[0])
        _, to_y = edge_span(-dy, brick[1], margins[1])

        @pl.when(jnp.logical_not(place.exists((dx, dy, 0))))
        def _():
            for ref in refs:
                for k in range(ref.shape[0]):
                    shape = (to_x.stop - to_x.start, to_y.stop - to_y.start, brick[2])
                    ref[k, to_x, to_y, lanes] = jnp.zeros(shape, F32)


def sweep_kernel(counts, brick, margins, forcing, start, modulus, zone_u, zone_w, *scratch):
    fields, rows_in, rows_out, sides = scratch[0:4], scratch[4], scratch[5], scratch[6:10]
    coupling, inverse = scratch[10:12]
    face_send, face_recv, bulk_send, bulk_recv, peer_send, peer_recv = scratch[12:]
    place = Place(counts)
    bx, by, bz = brick
    hx, hy = margins
    lanes = pl.ds(pl.multiple_of(place.here[2] * bz, bz), bz)
    row = iota((by, bz), 0)
    lane = iota((by, bz), 1)

    def stage(x, _):
        for k in range(3):
            u = start[k, x]
            fields[0][k, x + 1] = u
            rows_out[0, 0, k, pl.ds(x, 1), :] = u[:1]
            rows_out[0, 1, k, pl.ds(x, 1), :] = u[by - 1 :]
            zone_w[k, hx + x, hy : hy + by, lanes] = forcing[k, x]
        m = modulus[x]
        fields[0][3, x + 1] = m
        rows_out[0, 0, 3, pl.ds(x, 1), :] = m[:1]
        rows_out[0, 1, 3, pl.ds(x, 1), :] = m[by - 1 :]
        zone_w[3, hx + x, hy : hy + by, lanes] = m
        return 0

    lax.fori_loop(0, bx, stage, 0)

    def faces(sweep):
        channels = 4 if sweep == 0 else 3
        field = fields[sweep]
        messages = []
        for n, step in enumerate(FACES):
            dx, dy, dz = step
            if dx:
                source = field.at[:, bx if dx > 0 else 1]
                target = field.at[:, 0 if dx > 0 else bx + 1]
            elif dy:
                source = rows_out.at[sweep, 1 if dy > 0 else 0, :channels]
                target = rows_in.at[sweep, 0 if dy > 0 else 1, :channels]
            else:
                source = field.at[:, 1 : bx + 1]
                target = sides[sweep].at[0 if dz > 0 else 1]
            at = (sweep, n)
            messages.append(
                Message(place, step, source, target, face_send.at[at], face_recv.at[at])
            )
        return messages

    clear_outside(place, brick, margins, (zone_u, zone_w), lanes)
    for n, (dx, dy, dz) in enumerate(FACES):

        @pl.when(jnp.logical_not(place.exists((dx, dy, dz))))
        def _():
            for sweep in range(FSWEEPS):
                if dx:
                    plane = 0 if dx < 0 else bx + 1
                    for k in range(fields[sweep].shape[0]):
                        fields[sweep][k, plane] = jnp.zeros((by, bz), F32)
                elif dy:
                    for k in range(4):
                        rows_in[sweep, 0 if dy < 0 else 1, k] = jnp.zeros((bx, bz), F32)
                else:
                    for k in range(sides[sweep].shape[1]):
                        blank = jnp.zeros((bx, by, bz), F32)
                        sides[sweep][0 if dz < 0 else 1, k] = blank

    place.greet()
    messages = faces(0)
    pending = list(messages)
    for message in messages:
        message.start()
    bulk = spread_messages(
        place, brick, margins, zone_w, lanes, bulk_send.at[0], bulk_recv.at[0]
    )
    for message in bulk:
        message.start()

    def around(sweep, k, x, u):
        low, high = rows_in[sweep, 0, k, pl.ds(x, 1), :], rows_in[sweep, 1, k, pl.ds(x, 1), :]
        y_up = jnp.where(row == by - 1, jnp.broadcast_to(high, u.shape), roll(u, -1, 0))
        y_down = jnp.where(row == 0, jnp.broadcast_to(low, u.shape), roll(u, 1, 0))
        below, above = sides[sweep][0, k, x], sides[sweep][1, k, x]
        z_up = jnp.where(lane == bz - 1, roll(above, -1, 1), roll(u, -1, 1))
        z_down = jnp.where(lane == 0, roll(below, 1, 1), roll(u, 1, 1))
        field = fields[sweep]
        return field[k, x + 2], field[k, x], y_up, y_down, z_up, z_down

    def couple(x, _):
        m = fields[0][3, x + 1]
        below = MASS_TERM
        for n, other in enumerate(around(0, 3, x, m)):
            face = 0.5 * (m + other)
            coupling[n, x] = face
            below = below + face
        inverse[x] = 1.0 / below
        return 0

    for sweep in range(FSWEEPS):
        for message in messages:
            message.arrived()
        if sweep == 0:
            lax.fori_loop(0, bx, couple, 0)

        def relax(x, _, sweep=sweep):
            weights = [coupling[n, x] for n in range(6)]
            scale = inverse[x]
            for k in range(3):
                u = fields[sweep][k, x + 1]
                total = forcing[k, x]
                for weight, other in zip(weights, around(sweep, k, x, u)):
                    total = total + weight * other
                total = total * scale
                if sweep < FSWEEPS - 1:
                    fields[sweep + 1][k, x + 1] = total
                    rows_out[sweep + 1, 0, k, pl.ds(x, 1), :] = total[:1]
                    rows_out[sweep + 1, 1, k, pl.ds(x, 1), :] = total[by - 1 :]
                else:
                    zone_u[k, hx + x, hy : hy + by, lanes] = total
            return 0

        lax.fori_loop(0, bx, relax, 0)
        if sweep < FSWEEPS - 1:
            messages = faces(sweep + 1)
            pending += messages
            for message in messages:
                message.start()
    last = spread_messages(
        place, brick, margins, zone_u, lanes, bulk_send.at[1], bulk_recv.at[1]
    )
    for message in last:
        message.start()
    for message in bulk:
        message.arrived()
    copies = peer_copies(place, zone_w, lanes, peer_send.at[0], peer_recv.at[0])
    for copy in copies:
        copy.start()
    for message in last:
        message.arrived()
    more = peer_copies(place, zone_u, lanes, peer_send.at[1], peer_recv.at[1])
    for copy in more:
        copy.start()
    for message in pending + bulk + last:
        message.sent()
    for copy in copies + more:
        copy.wait()


def gather_kernel(counts, brick, margins, added, modulus, out, total, from_peer, *scratch):
    from_x, from_y, from_xy, send, recv, peer_send, peer_recv = scratch
    place = Place(counts)
    bx, by, bz = brick
    hx, hy = margins

    def part(turn):
        at = lax.rem(place.here[2] + turn, counts[2])
        return pl.ds(pl.multiple_of(at * bz, bz), bz)

    targets = {}
    for n, (dx, dy) in enumerate(AROUND):
        if dy == 0:
            targets[n] = from_x.at[(dx + 1) // 2]
        elif dx == 0:
            targets[n] = from_y.at[(dy + 1) // 2]
        else:
            targets[n] = from_xy.at[dx + 1 + (dy + 1) // 2]

        @pl.when(jnp.logical_not(place.exists((-dx, -dy, 0))))
        def _():
            targets[n][...] = jnp.zeros(targets[n].shape, F32)

    place.greet()
    copies = [
        pltpu.make_async_remote_copy(
            src_ref=added.at[:, :, part(turn)],
            dst_ref=from_peer.at[turn - 1],
            send_sem=peer_send.at[turn - 1],
            recv_sem=peer_recv.at[turn - 1],
            device_id=tuple(place.peer(turn)),
            device_id_type=MESH_ID,
        )
        for turn in range(1, counts[2])
    ]
    for copy in copies:
        copy.start()
    for copy in copies:
        copy.wait_recv()

    def collect(x, _):
        value = added[x, :, part(0)]
        for turn in range(1, counts[2]):
            value = value + from_peer[turn - 1, x]
        total[x] = value
        return 0

    lax.fori_loop(0, total.shape[0], collect, 0)
    messages = []
    for n, (dx, dy) in enumerate(AROUND):
        _, at_x = edge_span(-dx, bx, hx)
        _, at_y = edge_span(-dy, by, hy)
        messages.append(
            Message(place, (dx, dy, 0), total.at[at_x, at_y], targets[n], send.at[n], recv.at[n])
        )
    for message in messages:
        message.start()

    def centre(x, _):
        out[x] = modulus[x] + total[hx + x, hy : hy + by, :]
        return 0

    lax.fori_loop(0, bx, centre, 0)
    for message in messages:
        message.arrived()
    for n, (dx, dy) in enumerate(AROUND):
        to_x, _ = edge_span(-dx, bx, hx)
        to_y, _ = edge_span(-dy, by, hy)
        out[to_x.start - hx : to_x.stop - hx, to_y.start - hy : to_y.stop - hy, :] += targets[n][...]
    for message in messages:
        message.sent()
    for copy in copies:
        copy.wait_send()


FIELDS = 8


def coarse_fields(zone_u, zone_f, zone_m, temp, fields):
    rows = zone_m.shape[1]
    first_y = iota((rows, 128), 0) % 2 == 1
    first_z = iota((rows, 128), 1) % 2 == 1
    rank = iota((PC, 128), 0)
    lane = iota((PC, 128), 1)
    for x in range(PC):
        for k in range(3):
            sums = [None] * FIELDS

            def put(number, value):
                sums[number] = value if sums[number] is None else sums[number] + value

            for a in range(2):
                at = 2 * x + 1 + a
                u, m = zone_u[k, at], zone_m[at]
                applied = MASS_TERM * u
                laplace = jnp.zeros_like(u)
                for number, (axis, step) in enumerate(
                    ((0, 1), (0, -1), (1, 1), (1, -1), (2, 1), (2, -1))
                ):
                    if axis == 0:
                        u_next, m_next = zone_u[k, at + step], zone_m[at + step]
                    else:
                        u_next, m_next = roll(u, -step, axis - 1), roll(m, -step, axis - 1)
                    change = u - u_next
                    applied = applied + 0.5 * (m + m_next) * change
                    laplace = laplace + change
                    flow = -0.5 * m_next * change
                    if axis == 0:
                        same = (a == 0) == (step == 1)
                        put(0 if same else 1 + number, flow)
                    else:
                        first = first_y if axis == 1 else first_z
                        near = first if step == 1 else ~first
                        put(0, jnp.where(near, flow, 0.0))
                        put(1 + number, jnp.where(near, 0.0, flow))
                put(0, -0.5 * m * laplace)
                put(7, zone_f[k, at] - applied)
            for number in range(FIELDS):
                slot = temp.at[k * FIELDS + number]
                slot[...] = sums[number]
                pair = slot[pl.ds(1, PC, stride=2), :] + slot[pl.ds(2, PC, stride=2), :]
                pair = pair + roll(pair, -1, 1)
                keep = (lane % 2 == 1) & (lane < 2 * PC)
                if number == 1 and x == PC - 1 or number == 2 and x == 0:
                    keep = jnp.zeros_like(keep)
                if number == 3:
                    keep = keep & (rank < PC - 1)
                if number == 4:
                    keep = keep & (rank > 0)
                if number == 5:
                    keep = keep & (lane < 2 * PC - 2)
                if number == 6:
                    keep = keep & (lane > 1)
                fields[k * FIELDS + number, x * PC : (x + 1) * PC, :] = jnp.where(keep, pair, 0.0)


def assemble(fields, strip, mat, side):
    size = fields.shape[1]
    gap = iota((size, 128), 1) - iota((size, 128), 0)
    mat[...] = jnp.zeros_like(mat)
    side[...] = jnp.zeros_like(side)
    for c in range(2):
        for t in range(PC // 2):
            z = t if c == 0 else PC - 1 - t
            for k in range(3):
                def column(number):
                    value = fields[k * FIELDS + number, :, 2 * z + 1 : 2 * z + 2]
                    return jnp.broadcast_to(value, (size, 128))

                part = slice(k * size, (k + 1) * size)
                ahead, behind = (5, 6) if c == 0 else (6, 5)
                strip[part, 0:128] = jnp.where(gap == 0, column(behind), 0.0)
                inner = jnp.where(gap == 0, column(0), 0.0)
                for number, offset in ((1, PC), (2, -PC), (3, 1), (4, -1)):
                    inner = jnp.where(gap == offset, column(number), inner)
                strip[part, 128:256] = inner
                strip[part, 256:384] = jnp.where(gap == 0, column(ahead), 0.0)
                strip[part, 384:512] = column(7)
            product = dot(strip[:, :384], strip[...], (0, 0))
            for i in range(3):
                at = t - 1 + i
                if at < 0:
                    continue
                rows = slice(128 * i, 128 * (i + 1))
                mat[c, at] += product[rows, 128 * i : 128 * (i + 1)]
                for j in range(i + 1, 3):
                    place = slice(128 * (j - i - 1), 128 * (j - i))
                    side[c, at, :, place] += product[rows, 128 * j : 128 * (j + 1)]
                side[c, at, :, 256:384] += product[rows, 384:512]


def inverted(blocks, count):
    row_at = iota(blocks[0].shape, 0)
    lane_at = iota((1, blocks[0].shape[1]), 1)
    shape = blocks[0].shape
    for first in range(0, count, PANEL):
        pivots = range(first, min(first + PANEL, count))
        states = []
        for block in blocks:
            columns = [jnp.broadcast_to(block[:, j : j + 1], shape) for j in pivots]
            states.append([columns, [block[j : j + 1, :] for j in pivots], block])
        for i, j in enumerate(pivots):
            for state in states:
                columns, rows, block = state
                pivot = 1.0 / columns[i][j : j + 1, :]
                row = jnp.where(lane_at == j, pivot, rows[i] * pivot)
                column = jnp.where(row_at == j, -1.0, columns[i])
                for n in range(i + 1, len(columns)):
                    crossing = columns[n][j : j + 1, :] * pivot
                    rows[n] = jnp.where(lane_at == j, 0.0, rows[n])
                    rows[n] = rows[n] - columns[i][pivots[n] : pivots[n] + 1, :] * row
                    columns[n] = jnp.where(row_at == j, 0.0, columns[n]) - column * crossing
                clear = (row_at == j) | (lane_at == j)
                state[2] = jnp.where(clear, 0.0, block) - column * row
        blocks = [state[2] for state in states]
    return blocks


def eliminate(t, chains, size, ridge, mat, side, solved):
    params = PC * PC
    diagonal = (iota((size, 128), 0) == iota((size, 128), 1)) & (iota((size, 128), 0) < params)
    blocks = [mat[c, t, :size, :] + jnp.where(diagonal, ridge, 0.0) for c in chains]
    for c, inverse in zip(chains, inverted(blocks, params)):
        right = side[c, t]
        w = dot(inverse, right, (1, 0))
        solved[c, t] = w
        schur = dot(right[:size, :256], w, (0, 0))
        mat[c, t + 1] -= schur[:128, :128]
        side[c, t + 1, :, 0:128] -= schur[:128, 128:256]
        side[c, t + 1, :, 256:384] -= schur[:128, 256:384]
        mat[c, t + 2] -= schur[128:, 128:256]
        side[c, t + 2, :, 256:384] -= schur[128:, 256:384]


def solve_zone(fields, mat, side, solved, answer):
    size = fields.shape[1]
    squares = jnp.zeros((size, 128), F32)
    for number in range(3 * FIELDS):
        if number % FIELDS < FIELDS - 1:
            squares = squares + fields[number] * fields[number]
    trace = jnp.sum(jnp.sum(squares, axis=0, keepdims=True), axis=1, keepdims=True)
    ridge = DAMPING * trace / PC**3 + EPSILON
    meet = PC // 2 - 1

    def both(t, _):
        eliminate(t, (0, 1), size, ridge, mat, side, solved)
        return 0

    lax.fori_loop(0, meet, both, 0)
    mat[0, meet] += mat[1, meet + 1]
    mat[0, meet + 1] += mat[1, meet]
    side[0, meet, :, 0:128] += side[1, meet, :, 0:128].T
    side[0, meet, :, 256:384] += side[1, meet + 1, :, 256:384]
    side[0, meet + 1, :, 256:384] += side[1, meet, :, 256:384]

    def single(t, _):
        eliminate(t, (0,), size, ridge, mat, side, solved)
        return 0

    lax.fori_loop(meet, meet + 2, single, 0)
    answer[...] = jnp.zeros_like(answer)

    def back(t, c):
        value = solved[c, t, :, 256:384]
        value = value - dot(solved[c, t, :, 0:128], answer[c, t + 1], (1, 0))
        value = value - dot(solved[c, t, :, 128:256], answer[c, t + 2], (1, 0))
        answer[c, t, :size, :] = value

    answer[0, meet + 1, :size, :] = solved[0, meet + 1, :, 256:384]
    value = solved[0, meet, :, 256:384]
    answer[0, meet, :size, :] = value - dot(solved[0, meet, :, 0:128], answer[0, meet + 1], (1, 0))
    answer[1, meet] = answer[0, meet + 1]
    answer[1, meet + 1] = answer[0, meet]
    for t in range(meet - 1, -1, -1):
        for c in range(2):
            back(t, c)


def cut_zone(begin, depth, zone_all_u, zone_all_w, zone_u, zone_f, zone_m):
    count, rows = zone_m.shape[:2]
    whole_rows, whole_lanes = zone_all_u.shape[-2:]
    shift = lax.rem(whole_lanes - begin[2], whole_lanes)
    shift_y = lax.rem(whole_rows - begin[1], whole_rows)
    z = begin[2] + iota((rows, 128), 1)
    inside = (z >= 0) & (z < depth)

    def cut(x, _):
        def take(ref, k):
            plane = pltpu.roll(ref[k, begin[0] + x], shift, 1)[:, :128]
            return jnp.where(inside, pltpu.roll(plane, shift_y, 0)[:rows], 0.0)

        for k in range(3):
            zone_u[k, x] = take(zone_all_u, k)
            zone_f[k, x] = take(zone_all_w, k)
        zone_m[x] = take(zone_all_w, 3)
        return 0

    lax.fori_loop(0, count, cut, 0)


def place_zone(begin, zone_m, answer, spread, temp, added):
    rows = zone_m.shape[1]
    span = 2 * PC
    lane = iota((128, 128), 1)
    update = jnp.zeros((128, 128), F32)
    for z in range(PC):
        value = answer[0, z] if z < PC // 2 else answer[1, PC - 1 - z]
        update = jnp.where((lane == 2 * z + 1) | (lane == 2 * z + 2), -value, update)
    spread[...] = update

    def ramp(position):
        value = jnp.sin(math.pi * (position.astype(F32) - 0.5) / span)
        return jnp.where((position >= 1) & (position <= span), value, 0.0)

    weight = ramp(iota((rows, 128), 0)) * ramp(iota((rows, 128), 1))
    temp[0] = jnp.zeros_like(weight)
    shift = lax.rem(begin[2] + added.shape[2], added.shape[2])
    for x in range(PC):
        part = spread[x * PC : (x + 1) * PC, :]
        temp[0, pl.ds(1, PC, stride=2), :] = part
        temp[0, pl.ds(2, PC, stride=2), :] = part
        value = weight * temp[0]
        for a in range(2):
            at = 2 * x + 1 + a
            plane = value * math.sin(math.pi * (at - 0.5) / span) * zone_m[at]
            plane = jnp.pad(plane, ((0, added.shape[1] - rows), (0, 0)))
            plane = pltpu.roll(plane, begin[1], 0)
            plane = jnp.pad(plane, ((0, 0), (0, added.shape[2] - 128)))
            added[begin[0] + at] += pltpu.roll(plane, shift, 1)


def zone_kernel(counts, brick, margins, corners, zone_all_u, zone_all_w, field_out, added, *scratch):
    zone_u, zone_f, zone_m = scratch[:3]
    temp, fields, strip, mat, side, solved, answer, spread = scratch[3:]
    bx, by, bz = brick
    hx, hy = margins
    here = [lax.axis_index(name) for name in AXES]
    lanes = pl.ds(pl.multiple_of(here[2] * bz, bz), bz)
    for k in range(3):
        field_out[k] = zone_all_u[k, hx : hx + bx, hy : hy + by, lanes]
    added[...] = jnp.zeros_like(added)
    for number in range(corners.shape[0]):
        begin = [
            corners[number, 0] - here[0] * bx + hx - 1,
            corners[number, 1] - here[1] * by + hy - 1,
            corners[number, 2] - 1,
        ]
        cut_zone(begin, counts[2] * bz, zone_all_u, zone_all_w, zone_u, zone_f, zone_m)
        fields[...] = jnp.zeros_like(fields)
        coarse_fields(zone_u, zone_f, zone_m, temp, fields)
        assemble(fields, strip, mat, side)
        solve_zone(fields, mat, side, solved, answer)
        place_zone(begin, zone_m, answer, spread, temp, added)


def body(forcing, start_field, modulus, corners):
    brick = modulus.shape
    bx, by, bz = brick
    counts = [lax.axis_size(name) for name in AXES]
    margins = (HALO, -(-HALO // 8) * 8)
    span = [size + 2 * margin for size, margin in zip(brick, margins)] + [counts[2] * bz]
    whole = pl.BlockSpec(memory_space=pltpu.VMEM)
    dma = pltpu.SemaphoreType.DMA
    peers = max(counts[2] - 1, 1)
    zone_all_u, zone_all_w = pl.pallas_call(
        functools.partial(sweep_kernel, counts, brick, margins),
        out_shape=(
            jax.ShapeDtypeStruct((3, *span), F32),
            jax.ShapeDtypeStruct((4, *span), F32),
        ),
        in_specs=[whole, whole, whole],
        out_specs=(whole, whole),
        scratch_shapes=[
            pltpu.VMEM((4, bx + 2, by, bz), F32),
            *[pltpu.VMEM((3, bx + 2, by, bz), F32)] * (FSWEEPS - 1),
            pltpu.VMEM((FSWEEPS, 2, 4, bx, bz), F32),
            pltpu.VMEM((FSWEEPS, 2, 4, bx, bz), F32),
            pltpu.VMEM((2, 4, bx, by, bz), F32),
            *[pltpu.VMEM((2, 3, bx, by, bz), F32)] * (FSWEEPS - 1),
            pltpu.VMEM((6, bx, by, bz), F32),
            pltpu.VMEM((bx, by, bz), F32),
            dma((FSWEEPS, len(FACES))),
            dma((FSWEEPS, len(FACES))),
            dma((2, len(AROUND))),
            dma((2, len(AROUND))),
            dma((2, peers)),
            dma((2, peers)),
        ],
        compiler_params=pltpu.CompilerParams(
            collective_id=0, has_side_effects=True, vmem_limit_bytes=40 * 1024 * 1024
        ),
        name="sweeps",
    )(forcing, start_field, modulus)
    zone_span = 2 * PC + 2
    zone_rows = -(-zone_span // 8) * 8
    size = -(-PC * PC // 8) * 8
    planes = PC // 2 + 3
    field, added = pl.pallas_call(
        functools.partial(zone_kernel, counts, brick, margins),
        out_shape=(
            jax.ShapeDtypeStruct(forcing.shape, F32),
            jax.ShapeDtypeStruct(tuple(span), F32),
        ),
        in_specs=[pl.BlockSpec(memory_space=pltpu.SMEM), whole, whole],
        out_specs=(whole, whole),
        scratch_shapes=[
            pltpu.VMEM((3, zone_span, zone_rows, 128), F32),
            pltpu.VMEM((3, zone_span, zone_rows, 128), F32),
            pltpu.VMEM((zone_span, zone_rows, 128), F32),
            pltpu.VMEM((3 * FIELDS, zone_rows, 128), F32),
            pltpu.VMEM((3 * FIELDS, size, 128), F32),
            pltpu.VMEM((3 * size, 512), F32),
            pltpu.VMEM((2, planes, 128, 128), F32),
            pltpu.VMEM((2, planes, 128, 384), F32),
            pltpu.VMEM((2, planes, size, 384), F32),
            pltpu.VMEM((2, planes, 128, 128), F32),
            pltpu.VMEM((128, 128), F32),
        ],
        compiler_params=pltpu.CompilerParams(vmem_limit_bytes=40 * 1024 * 1024),
        name="zone",
    )(corners, zone_all_u, zone_all_w)
    updated = pl.pallas_call(
        functools.partial(gather_kernel, counts, brick, margins),
        out_shape=jax.ShapeDtypeStruct(brick, F32),
        in_specs=[whole, whole],
        out_specs=whole,
        scratch_shapes=[
            pltpu.VMEM((span[0], span[1], bz), F32),
            pltpu.VMEM((peers, span[0], span[1], bz), F32),
            pltpu.VMEM((2, margins[0], by, bz), F32),
            pltpu.VMEM((2, bx, margins[1], bz), F32),
            pltpu.VMEM((4, margins[0], margins[1], bz), F32),
            dma((len(AROUND),)),
            dma((len(AROUND),)),
            dma((peers,)),
            dma((peers,)),
        ],
        compiler_params=pltpu.CompilerParams(
            collective_id=1, has_side_effects=True, vmem_limit_bytes=40 * 1024 * 1024
        ),
        name="gather",
    )(added, modulus)
    return (field, updated)


def solution(mesh):
    placed = (
        P(None, "gx", "gy", "gz"),
        P(None, "gx", "gy", "gz"),
        P("gx", "gy", "gz"),
        P(("gx", "gy", "gz"), None),
    )
    return jax.shard_map(
        body,
        mesh=mesh,
        in_specs=placed,
        out_specs=(P(None, "gx", "gy", "gz"), P("gx", "gy", "gz")),
        check_vma=False,
    )
```

time: 217 us -> 139 us (0.64)
  waiting for transfers between devices: 63 us -> 0 us
  starting transfers between devices: 31.6 us -> 0 us
  Pallas kernels: 103 us -> 133 us
  other arithmetic: 11.7 us -> 0 us
    ppermute x14 -> x0, waiting for transfers between devices: 63 us -> none  [the longest x4 25.3 us: exchange(): lax.ppermute(first, axis, backward)]
    ppermute x14 -> x0, starting transfers between devices: 31.6 us -> none  [the longest x4 14.4 us: exchange(): lax.ppermute(last, axis, forward)]
    pallas_call x2 -> x3, Pallas kernels: 103 us -> 133 us  [the longest x1 65.4 us: body(): pl.pallas_call(functools.partial(zone_kernel, counts, brick, margins), ou...]
    concatenate x2 -> x0, other arithmetic: 8.78 us -> none  [the longest x1 7.53 us: body(): jnp.concatenate([jnp.concatenate([low_ends[0], x_low, low_ends[1]], axis=...]
    slice x11 -> x0, local copies, waits for them, and re-layouts: 4.02 us -> none  [the longest x3 1.17 us: pack_margins(): lax.slice_in_dim(values, inner + margin, inner + 2 * margin, axis=which_a...]
    unnamed x12 -> x9, local copies, waits for them, and re-layouts: 0.8 us -> 4.2 us
  transfers between devices with their start and end apart: 14 -> 0, of which waited for: 12 -> 0; matrix products, arithmetic and copies ran while one was open for 2% -> 0% of each run, Pallas kernels for 0% -> 0%
where the time goes in v1:
time: 139 us; the launch traced here: 138 us
  Pallas kernels  133 us (96%)
  local copies, waits for them, and re-layouts  4.2 us (3%)
    pallas_call x1, Pallas kernels, body(): pl.pallas_call(functools.partial(zone_kernel, counts, brick, margins), ou...  65.4 us
    pallas_call x1, Pallas kernels, body(): pl.pallas_call(functools.partial(sweep_kernel, counts, brick, margins), o...  52.7 us
    pallas_call x1, Pallas kernels, body(): pl.pallas_call(functools.partial(gather_kernel, counts, brick, margins),...  14.9 us
    unnamed x9, local copies, waits for them, and re-layouts  4.2 us

profile of v1, /device:TPU:0, one launch (start us, length us, event | category | flops | bytes accessed | tf_op | source)
XLA Modules:
  0.0 137.9 jit_solution(15004914150760572768)
XLA Ops:
  0.6 0.0 copy-start
  0.6 0.9 copy-done
  1.5 0.0 copy-start.1
  1.5 1.0 copy-done.1
  2.5 0.0 copy-start.2
  2.5 1.0 copy-done.2
  3.5 52.7 %sweeps.1 = (f32[3,28,32,256]{3,2,1,0:T(8,128)S(1)}, f32[4,28,32,256]{3,2,1,0:T(8,128)S(1)}) custom-call(f32[3,16,16,128]{3,2,1,0:T(8,128)S(1)} %copy-done.1, f32[3,16,16,128]{3,2,1,0:T(8,128)S(1)} %copy-done.2, f32[16,16,128]{2,1,0:T(8,128)S(1)} %copy-done), custom_call_target="tpu_custom_call" | custom-call | tf_op jit(solution)/shard_map/sweeps/pallas_call | solution.py:653
  56.3 0.0 copy-start.3
  56.3 0.6 copy-done.3
  56.9 65.4 %zone.1 = (f32[3,16,16,128]{3,2,1,0:T(8,128)}, f32[28,32,256]{2,1,0:T(8,128)S(1)}) custom-call(s32[1,3]{1,0:T(1,128)S(1)} %copy-done.3, f32[3,28,32,256]{3,2,1,0:T(8,128)S(1)} %get-tuple-element.6.zone_all_u, f32[4,28,32,256]{3,2,1,0:T(8,128)S(1)} %get-tuple-element.7.zone_all_w), custom_call_target="tpu_custom_call" | custom-call | tf_op jit(solution)/shard_map/zone/pallas_call | solution.py:686
  122.3 14.9 %gather.1 = f32[16,16,128]{2,1,0:T(8,128)S(1)} custom-call(f32[28,32,256]{2,1,0:T(8,128)S(1)} %get-tuple-element.9.added, f32[16,16,128]{2,1,0:T(8,128)S(1)} %copy-done), custom_call_target="tpu_custom_call" | custom-call | tf_op jit(solution)/shard_map/gather/pallas_call | solution.py:710
  137.2 0.7 copy.7
Async XLA Ops:
  0.6 0.9 copy-start
  1.5 1.0 copy-start.1
  2.5 1.0 copy-start.2
  56.3 0.7 copy-start.3

commit v2 on v1

--- a/solution.py
+++ b/solution.py
@@ -17,7 +17,6 @@
 DAMPING = 0.1
 EPSILON = 1e-06
 HIGHEST = lax.Precision.HIGHEST
-PANEL = 2
 F32 = jnp.float32
 
 
@@ -106,19 +105,21 @@
         pl.when(self.place.exists(opposite(self.step)))(self.copy.wait_recv)
 
 
-def edge_span(move, size, margin):
+def edge_span(move, size, margin, reach=None):
+    reach = margin if reach is None else reach
     if move > 0:
-        return slice(size, size + margin), slice(0, margin)
+        return slice(margin + size - reach, margin + size), slice(margin - reach, margin)
     if move < 0:
-        return slice(margin, 2 * margin), slice(margin + size, 2 * margin + size)
+        far = margin + size
+        return slice(margin, margin + reach), slice(far, far + reach)
     return slice(margin, margin + size), slice(margin, margin + size)
 
 
 def spread_messages(place, brick, margins, ref, lanes, send, recv):
     messages = []
     for n, (dx, dy) in enumerate(AROUND):
-        from_x, to_x = edge_span(dx, brick[0], margins[0])
-        from_y, to_y = edge_span(dy, brick[1], margins[1])
+        from_x, to_x = edge_span(dx, brick[0], margins[0], HALO)
+        from_y, to_y = edge_span(dy, brick[1], margins[1], HALO)
         messages.append(
             Message(
                 place,
@@ -442,159 +443,226 @@
                 fields[k * FIELDS + number, x * PC : (x + 1) * PC, :] = jnp.where(keep, pair, 0.0)
 
 
-def assemble(fields, strip, mat, side):
+PAIRS = ((0, 0, 0), (1, 0, 0), (-1, 0, 0), (0, 1, 0), (0, -1, 0), (0, 0, 1), (0, 0, -1))
+BANDS = tuple(
+    sorted({tuple(b - a for a, b in zip(one, two)) for one in PAIRS for two in PAIRS})
+)
+PER_GROUP = 12
+
+
+def transpose_fields(fields, packed, flat):
     size = fields.shape[1]
-    gap = iota((size, 128), 1) - iota((size, 128), 0)
+    flat[...] = jnp.zeros_like(flat)
+    for group in range(2):
+        total = None
+        for j in range(PER_GROUP):
+            shift = 2 * PC * (j // 2) - 1 + j % 2
+            part = fields[group * PER_GROUP + j]
+            part = roll(part, shift, 1) if shift else part
+            total = part if total is None else total + part
+        packed[:size, :] = total
+        packed[size:, :] = jnp.zeros((128 - size, 128), F32)
+        packed[...] = packed[...].T
+        for j in range(PER_GROUP):
+            first = 2 * PC * (j // 2) + j % 2
+            flat[group * PER_GROUP + j, :PC, :] = packed[pl.ds(first, PC, stride=2), :]
+
+
+def band_sums(flat, packed, bands, slopes):
+    columns = [[flat[k * FIELDS + n] for k in range(3)] for n in range(FIELDS)]
+
+    def product(a, b):
+        return sum(columns[a][k] * columns[b][k] for k in range(3))
+
+    def moved(value, step):
+        x, y, z = step
+        value = roll(value, PC * x + y, 1) if x or y else value
+        return roll(value, z, 0) if z else value
+
+    totals = {}
+    trace = None
+    for a in range(len(PAIRS)):
+        for b in range(a, len(PAIRS)):
+            value = product(a, b)
+            if a == b:
+                trace = value if trace is None else trace + value
+            for one, two in {(a, b), (b, a)}:
+                key = tuple(q - p for p, q in zip(PAIRS[one], PAIRS[two]))
+                part = moved(value, PAIRS[two])
+                totals[key] = part if key not in totals else totals[key] + part
+    trace = jnp.sum(jnp.sum(trace, axis=0, keepdims=True), axis=1, keepdims=True)
+    ridge = DAMPING * trace / PC**3 + EPSILON
+    totals[0, 0, 0] = totals[0, 0, 0] + ridge
+    for n, key in enumerate(BANDS):
+        bands[n] = totals[key]
+    slope = None
+    for a in range(len(PAIRS)):
+        part = moved(product(a, FIELDS - 1), PAIRS[a])
+        slope = part if slope is None else slope + part
+    packed[...] = jnp.zeros_like(packed)
+    packed[: slope.shape[0], :] = slope
+    slopes[...] = packed[...].T
+
+
+def fill(c, t, z, bands, slopes, mat, side, reach):
+    params = PC * PC
+    lane = iota((8, 128), 1)
+    gap = lane - iota((8, 128), 0)
+    column = pltpu.roll(slopes[...], params - z, 1)
+    ahead = 1 if c == 0 else -1
+
+    def rows_of(depth):
+        found = []
+        for n, (x, y, dz) in enumerate(BANDS):
+            if dz == depth * ahead:
+                row = bands[n, pl.ds(z + depth * ahead, 1), :]
+                found.append((PC * x + y, jnp.broadcast_to(row, (8, 128))))
+        return found
+
+    parts = [rows_of(depth) for depth in range(reach + 1)]
+    for q in range(-(-params // 8)):
+        here = slice(8 * q, 8 * q + 8)
+        inside = lane < params
+
+        def block(entries):
+            value = jnp.zeros((8, 128), F32)
+            for offset, row in entries:
+                value = jnp.where(gap == 8 * q + offset, row, value)
+            return jnp.where(inside, value, 0.0)
+
+        mat[c, t, here, :] = block(parts[0])
+        first = block(parts[1]) if reach > 0 else jnp.zeros((8, 128), F32)
+        side[c, t, here, 0:128] = jnp.where(lane == params, column[here], first)
+        if reach > 1:
+            side[c, t, here, 128:256] = block(parts[2])
+
+
+def assemble(bands, slopes, mat, side):
+    meet = PC // 2 - 1
     mat[...] = jnp.zeros_like(mat)
     side[...] = jnp.zeros_like(side)
-    for c in range(2):
-        for t in range(PC // 2):
-            z = t if c == 0 else PC - 1 - t
-            for k in range(3):
-                def column(number):
-                    value = fields[k * FIELDS + number, :, 2 * z + 1 : 2 * z + 2]
-                    return jnp.broadcast_to(value, (size, 128))
-
-                part = slice(k * size, (k + 1) * size)
-                ahead, behind = (5, 6) if c == 0 else (6, 5)
-                strip[part, 0:128] = jnp.where(gap == 0, column(behind), 0.0)
-                inner = jnp.where(gap == 0, column(0), 0.0)
-                for number, offset in ((1, PC), (2, -PC), (3, 1), (4, -1)):
-                    inner = jnp.where(gap == offset, column(number), inner)
-                strip[part, 128:256] = inner
-                strip[part, 256:384] = jnp.where(gap == 0, column(ahead), 0.0)
-                strip[part, 384:512] = column(7)
-            product = dot(strip[:, :384], strip[...], (0, 0))
-            for i in range(3):
-                at = t - 1 + i
-                if at < 0:
-                    continue
-                rows = slice(128 * i, 128 * (i + 1))
-                mat[c, at] += product[rows, 128 * i : 128 * (i + 1)]
-                for j in range(i + 1, 3):
-                    place = slice(128 * (j - i - 1), 128 * (j - i))
-                    side[c, at, :, place] += product[rows, 128 * j : 128 * (j + 1)]
-                side[c, at, :, 256:384] += product[rows, 384:512]
-
-
-def inverted(blocks, count):
-    row_at = iota(blocks[0].shape, 0)
-    lane_at = iota((1, blocks[0].shape[1]), 1)
-    shape = blocks[0].shape
-    for first in range(0, count, PANEL):
-        pivots = range(first, min(first + PANEL, count))
-        states = []
-        for block in blocks:
-            columns = [jnp.broadcast_to(block[:, j : j + 1], shape) for j in pivots]
-            states.append([columns, [block[j : j + 1, :] for j in pivots], block])
-        for i, j in enumerate(pivots):
-            for state in states:
-                columns, rows, block = state
-                pivot = 1.0 / columns[i][j : j + 1, :]
-                row = jnp.where(lane_at == j, pivot, rows[i] * pivot)
-                column = jnp.where(row_at == j, -1.0, columns[i])
-                for n in range(i + 1, len(columns)):
-                    crossing = columns[n][j : j + 1, :] * pivot
-                    rows[n] = jnp.where(lane_at == j, 0.0, rows[n])
-                    rows[n] = rows[n] - columns[i][pivots[n] : pivots[n] + 1, :] * row
-                    columns[n] = jnp.where(row_at == j, 0.0, columns[n]) - column * crossing
-                clear = (row_at == j) | (lane_at == j)
-                state[2] = jnp.where(clear, 0.0, block) - column * row
-        blocks = [state[2] for state in states]
-    return blocks
-
-
-def eliminate(t, chains, size, ridge, mat, side, solved):
+
+    def both(t, _):
+        fill(0, t, t, bands, slopes, mat, side, 2)
+        fill(1, t, PC - 1 - t, bands, slopes, mat, side, 2)
+        return 0
+
+    lax.fori_loop(0, meet, both, 0)
+    fill(0, meet, meet, bands, slopes, mat, side, 1)
+    fill(0, meet + 1, meet + 1, bands, slopes, mat, side, 0)
+
+
+def factored(blocks, count):
+    lane = iota((8, 128), 1)
+    sub = iota((8, 128), 0)
+    tiles = -(-count // 8)
+
+    def over_lanes(value, at):
+        return jnp.broadcast_to(value[:, at : at + 1], value.shape)
+
+    def over_rows(value, at):
+        return jnp.broadcast_to(value[at : at + 1, :], value.shape)
+
+    grids = [[block[8 * q : 8 * q + 8] for q in range(tiles)] for block in blocks]
+    lower = [[] for _ in blocks]
+    scaled = [[] for _ in blocks]
+    for p in range(tiles):
+        pivots = range(8 * p, min(8 * p + 8, count))
+        within = (lane >= pivots[0]) & (lane <= pivots[-1])
+        keep = (lane <= pivots[-1]) & (sub < len(pivots))
+        for grid, low, high in zip(grids, lower, scaled):
+            panel = grid[p]
+            unit = jnp.where(lane - 8 * p == sub, 1.0, 0.0)
+            low.append(jnp.where(keep, jnp.where(within, unit, panel), 0.0))
+            columns = [over_lanes(panel, j) for j in pivots]
+            for i, j in enumerate(pivots):
+                column = columns[i]
+                pivot = 1.0 / over_rows(column, i)
+                row = jnp.where(lane == j, pivot, over_rows(panel, i) * pivot)
+                for n in range(i + 1, len(pivots)):
+                    crossing = over_rows(columns[n], i) * pivot
+                    columns[n] = jnp.where(sub == i, crossing, columns[n] - column * crossing)
+                cleared = jnp.where(lane == j, 0.0, panel)
+                panel = jnp.where(sub == i, row, cleared - column * row)
+            high.append(jnp.where(keep, panel, 0.0))
+            rows = [over_rows(panel, i) for i in range(len(pivots))]
+            for q in range(p + 1, tiles):
+                old = grid[q]
+                terms = [over_lanes(old, j) * row for j, row in zip(pivots, rows)]
+                while len(terms) > 1:
+                    pairs = [terms[n] + terms[n + 1] for n in range(0, len(terms) - 1, 2)]
+                    terms = pairs + terms[len(terms) - len(terms) % 2 :]
+                grid[q] = jnp.where(within, 0.0, old) - terms[0]
+    return [
+        (jnp.concatenate(low, axis=0), jnp.concatenate(high, axis=0))
+        for low, high in zip(lower, scaled)
+    ]
+
+
+def eliminate(t, chains, size, mat, side, lowers, solved, more=True):
     params = PC * PC
-    diagonal = (iota((size, 128), 0) == iota((size, 128), 1)) & (iota((size, 128), 0) < params)
-    blocks = [mat[c, t, :size, :] + jnp.where(diagonal, ridge, 0.0) for c in chains]
-    for c, inverse in zip(chains, inverted(blocks, params)):
-        right = side[c, t]
-        w = dot(inverse, right, (1, 0))
-        solved[c, t] = w
-        schur = dot(right[:size, :256], w, (0, 0))
-        mat[c, t + 1] -= schur[:128, :128]
-        side[c, t + 1, :, 0:128] -= schur[:128, 128:256]
-        side[c, t + 1, :, 256:384] -= schur[:128, 256:384]
-        mat[c, t + 2] -= schur[128:, 128:256]
-        side[c, t + 2, :, 256:384] -= schur[128:, 256:384]
-
-
-def solve_zone(fields, mat, side, solved, answer):
-    size = fields.shape[1]
-    squares = jnp.zeros((size, 128), F32)
-    for number in range(3 * FIELDS):
-        if number % FIELDS < FIELDS - 1:
-            squares = squares + fields[number] * fields[number]
-    trace = jnp.sum(jnp.sum(squares, axis=0, keepdims=True), axis=1, keepdims=True)
-    ridge = DAMPING * trace / PC**3 + EPSILON
+    mark = iota((128, 128), 1) == params
+    blocks = [mat[c, t, :size, :] for c in chains]
+    for c, (low, high) in zip(chains, factored(blocks, params)):
+        lowers[c, t, :size, :] = low
+        right = side[c, t, :size, :]
+        z = dot(high[:, :size], right, (1, 0))
+        solved[c, t, :size, :] = z
+        if not more:
+            continue
+        y = dot(low[:, :size], right, (1, 0))
+        schur = dot(y, z, (0, 0))
+        near, far = schur[:128], schur[128:]
+        mat[c, t + 1] -= near[:, :128]
+        side[c, t + 1, :, 0:128] -= jnp.where(mark, near[:, :128], near[:, 128:])
+        mat[c, t + 2] -= far[:, 128:]
+        side[c, t + 2, :, 0:128] -= jnp.where(mark, far[:, :128], 0.0)
+
+
+def solve_zone(size, mat, side, lowers, solved, spread):
+    params = PC * PC
     meet = PC // 2 - 1
+    mark = iota((128, 128), 1) == params
+    lowers[...] = jnp.zeros_like(lowers)
+    solved[...] = jnp.zeros_like(solved)
 
     def both(t, _):
-        eliminate(t, (0, 1), size, ridge, mat, side, solved)
+        eliminate(t, (0, 1), size, mat, side, lowers, solved)
         return 0
 
     lax.fori_loop(0, meet, both, 0)
     mat[0, meet] += mat[1, meet + 1]
     mat[0, meet + 1] += mat[1, meet]
-    side[0, meet, :, 0:128] += side[1, meet, :, 0:128].T
-    side[0, meet, :, 256:384] += side[1, meet + 1, :, 256:384]
-    side[0, meet + 1, :, 256:384] += side[1, meet, :, 256:384]
-
-    def single(t, _):
-        eliminate(t, (0,), size, ridge, mat, side, solved)
-        return 0
-
-    lax.fori_loop(meet, meet + 2, single, 0)
-    answer[...] = jnp.zeros_like(answer)
-
-    def back(t, c):
-        value = solved[c, t, :, 256:384]
-        value = value - dot(solved[c, t, :, 0:128], answer[c, t + 1], (1, 0))
-        value = value - dot(solved[c, t, :, 128:256], answer[c, t + 2], (1, 0))
-        answer[c, t, :size, :] = value
-
-    answer[0, meet + 1, :size, :] = solved[0, meet + 1, :, 256:384]
-    value = solved[0, meet, :, 256:384]
-    answer[0, meet, :size, :] = value - dot(solved[0, meet, :, 0:128], answer[0, meet + 1], (1, 0))
-    answer[1, meet] = answer[0, meet + 1]
-    answer[1, meet + 1] = answer[0, meet]
+    turned = side[1, meet, :, 0:128].T
+    side[0, meet, :, 0:128] += jnp.where(mark, side[1, meet + 1, :, 0:128], turned)
+    side[0, meet + 1, :, 0:128] += jnp.where(mark, side[1, meet, :, 0:128], 0.0)
+    eliminate(meet, (0,), size, mat, side, lowers, solved)
+    eliminate(meet + 1, (0,), size, mat, side, lowers, solved, more=False)
+
+    flag = iota((8, 128), 1) == params
+
+    def back(c, t, near, far):
+        row = jnp.concatenate([jnp.where(flag, -1.0, near), far], axis=1)
+        value = dot(row, solved[c, t], (1, 1))
+        return -dot(value, lowers[c, t], (1, 0))
+
+    blank = jnp.zeros((8, 128), F32)
+    rows = [blank] * PC
+    rows[meet + 1] = back(0, meet + 1, blank, blank)
+    rows[meet] = back(0, meet, rows[meet + 1], blank)
     for t in range(meet - 1, -1, -1):
-        for c in range(2):
-            back(t, c)
-
-
-def cut_zone(begin, depth, zone_all_u, zone_all_w, zone_u, zone_f, zone_m):
-    count, rows = zone_m.shape[:2]
-    whole_rows, whole_lanes = zone_all_u.shape[-2:]
-    shift = lax.rem(whole_lanes - begin[2], whole_lanes)
-    shift_y = lax.rem(whole_rows - begin[1], whole_rows)
-    z = begin[2] + iota((rows, 128), 1)
-    inside = (z >= 0) & (z < depth)
-
-    def cut(x, _):
-        def take(ref, k):
-            plane = pltpu.roll(ref[k, begin[0] + x], shift, 1)[:, :128]
-            return jnp.where(inside, pltpu.roll(plane, shift_y, 0)[:rows], 0.0)
-
-        for k in range(3):
-            zone_u[k, x] = take(zone_all_u, k)
-            zone_f[k, x] = take(zone_all_w, k)
-        zone_m[x] = take(zone_all_w, 3)
-        return 0
-
-    lax.fori_loop(0, count, cut, 0)
-
-
-def place_zone(begin, zone_m, answer, spread, temp, added):
+        rows[t] = back(0, t, rows[t + 1], rows[t + 2])
+        z = PC - 1 - t
+        rows[z] = back(1, t, rows[z - 1], rows[z - 2])
+    spread[...] = jnp.zeros_like(spread)
+    for z in range(PC):
+        spread[2 * z + 1 : 2 * z + 3, :] = -rows[z][:2]
+    spread[...] = spread[...].T
+
+
+def place_zone(begin, zone_m, spread, temp, added):
     rows = zone_m.shape[1]
     span = 2 * PC
-    lane = iota((128, 128), 1)
-    update = jnp.zeros((128, 128), F32)
-    for z in range(PC):
-        value = answer[0, z] if z < PC // 2 else answer[1, PC - 1 - z]
-        update = jnp.where((lane == 2 * z + 1) | (lane == 2 * z + 2), -value, update)
-    spread[...] = update
 
     def ramp(position):
         value = jnp.sin(math.pi * (position.astype(F32) - 0.5) / span)
@@ -617,9 +685,31 @@
             added[begin[0] + at] += pltpu.roll(plane, shift, 1)
 
 
+def cut_zone(begin, depth, zone_all_u, zone_all_w, zone_u, zone_f, zone_m):
+    count, rows = zone_m.shape[:2]
+    whole_rows, whole_lanes = zone_all_u.shape[-2:]
+    shift = lax.rem(whole_lanes - begin[2], whole_lanes)
+    shift_y = lax.rem(whole_rows - begin[1], whole_rows)
+    z = begin[2] + iota((rows, 128), 1)
+    inside = (z >= 0) & (z < depth)
+
+    def cut(x, _):
+        def take(ref, k):
+            plane = pltpu.roll(ref[k, begin[0] + x], shift, 1)[:, :128]
+            return jnp.where(inside, pltpu.roll(plane, shift_y, 0)[:rows], 0.0)
+
+        for k in range(3):
+            zone_u[k, x] = take(zone_all_u, k)
+            zone_f[k, x] = take(zone_all_w, k)
+        zone_m[x] = take(zone_all_w, 3)
+        return 0
+
+    lax.fori_loop(0, count, cut, 0)
+
+
 def zone_kernel(counts, brick, margins, corners, zone_all_u, zone_all_w, field_out, added, *scratch):
     zone_u, zone_f, zone_m = scratch[:3]
-    temp, fields, strip, mat, side, solved, answer, spread = scratch[3:]
+    temp, fields, packed, flat, bands, slopes, mat, side, lowers, solved, spread = scratch[3:]
     bx, by, bz = brick
     hx, hy = margins
     here = [lax.axis_index(name) for name in AXES]
@@ -636,9 +726,11 @@
         cut_zone(begin, counts[2] * bz, zone_all_u, zone_all_w, zone_u, zone_f, zone_m)
         fields[...] = jnp.zeros_like(fields)
         coarse_fields(zone_u, zone_f, zone_m, temp, fields)
-        assemble(fields, strip, mat, side)
-        solve_zone(fields, mat, side, solved, answer)
-        place_zone(begin, zone_m, answer, spread, temp, added)
+        transpose_fields(fields, packed, flat)
+        band_sums(flat, packed, bands, slopes)
+        assemble(bands, slopes, mat, side)
+        solve_zone(fields.shape[1], mat, side, lowers, solved, spread)
+        place_zone(begin, zone_m, spread, temp, added)
 
 
 def body(forcing, start_field, modulus, corners):
@@ -697,11 +789,14 @@
             pltpu.VMEM((zone_span, zone_rows, 128), F32),
             pltpu.VMEM((3 * FIELDS, zone_rows, 128), F32),
             pltpu.VMEM((3 * FIELDS, size, 128), F32),
-            pltpu.VMEM((3 * size, 512), F32),
+            pltpu.VMEM((128, 128), F32),
+            pltpu.VMEM((3 * FIELDS, 16, 128), F32),
+            pltpu.VMEM((len(BANDS), 16, 128), F32),
+            pltpu.VMEM((128, 128), F32),
             pltpu.VMEM((2, planes, 128, 128), F32),
-            pltpu.VMEM((2, planes, 128, 384), F32),
-            pltpu.VMEM((2, planes, size, 384), F32),
+            pltpu.VMEM((2, planes, 128, 256), F32),
             pltpu.VMEM((2, planes, 128, 128), F32),
+            pltpu.VMEM((2, planes, 128, 256), F32),
             pltpu.VMEM((128, 128), F32),
         ],
         compiler_params=pltpu.CompilerParams(vmem_limit_bytes=40 * 1024 * 1024),

time: 139 us -> 110 us (0.79)
  Pallas kernels: 133 us -> 103 us
    pallas_call x1, Pallas kernels: 65.4 us -> 44.4 us  [body(): pl.pallas_call(functools.partial(zone_kernel, counts, brick, margins), ou...]
    pallas_call x1, Pallas kernels: 52.7 us -> 45.9 us  [body(): pl.pallas_call(functools.partial(sweep_kernel, counts, brick, margins), o...]
    pallas_call x1, Pallas kernels: 14.9 us -> 13.1 us  [body(): pl.pallas_call(functools.partial(gather_kernel, counts, brick, margins),...]
where the time goes in v2:
time: 110 us; the launch traced here: 108 us
  Pallas kernels  103 us (94%)
  local copies, waits for them, and re-layouts  4.2 us (4%)
    pallas_call x1, Pallas kernels, body(): pl.pallas_call(functools.partial(sweep_kernel, counts, brick, margins), o...  45.9 us
    pallas_call x1, Pallas kernels, body(): pl.pallas_call(functools.partial(zone_kernel, counts, brick, margins), ou...  44.4 us
    pallas_call x1, Pallas kernels, body(): pl.pallas_call(functools.partial(gather_kernel, counts, brick, margins),...  13.1 us
    unnamed x9, local copies, waits for them, and re-layouts  4.2 us

profile of v2, /device:TPU:0, one launch (start us, length us, event | category | flops | bytes accessed | tf_op | source)
XLA Modules:
  0.0 108.3 jit_solution(1361208710473568822)
XLA Ops:
  0.6 0.0 copy-start
  0.6 0.9 copy-done
  1.5 0.0 copy-start.1
  1.5 1.0 copy-done.1
  2.5 0.0 copy-start.2
  2.5 1.0 copy-done.2
  3.5 45.9 %sweeps.1 = (f32[3,28,32,256]{3,2,1,0:T(8,128)S(1)}, f32[4,28,32,256]{3,2,1,0:T(8,128)S(1)}) custom-call(f32[3,16,16,128]{3,2,1,0:T(8,128)S(1)} %copy-done.1, f32[3,16,16,128]{3,2,1,0:T(8,128)S(1)} %copy-done.2, f32[16,16,128]{2,1,0:T(8,128)S(1)} %copy-done), custom_call_target="tpu_custom_call" | custom-call | tf_op jit(solution)/shard_map/sweeps/pallas_call | solution.py:745
  49.4 0.0 copy-start.3
  49.5 0.6 copy-done.3
  50.1 44.4 %zone.1 = (f32[3,16,16,128]{3,2,1,0:T(8,128)}, f32[28,32,256]{2,1,0:T(8,128)S(1)}) custom-call(s32[1,3]{1,0:T(1,128)S(1)} %copy-done.3, f32[3,28,32,256]{3,2,1,0:T(8,128)S(1)} %get-tuple-element.6.zone_all_u, f32[4,28,32,256]{3,2,1,0:T(8,128)S(1)} %get-tuple-element.7.zone_all_w), custom_call_target="tpu_custom_call" | custom-call | tf_op jit(solution)/shard_map/zone/pallas_call | solution.py:778
  94.5 13.1 %gather.1 = f32[16,16,128]{2,1,0:T(8,128)S(1)} custom-call(f32[28,32,256]{2,1,0:T(8,128)S(1)} %get-tuple-element.9.added, f32[16,16,128]{2,1,0:T(8,128)S(1)} %copy-done), custom_call_target="tpu_custom_call" | custom-call | tf_op jit(solution)/shard_map/gather/pallas_call | solution.py:805
  107.7 0.7 copy.7
Async XLA Ops:
  0.6 0.9 copy-start
  1.5 1.0 copy-start.1
  2.5 1.0 copy-start.2
  49.4 0.7 copy-start.3

commit v3 on v2

--- a/solution.py
+++ b/solution.py
@@ -59,7 +59,7 @@
     def peer(self, turn):
         return self.here[:2] + [lax.rem(self.here[2] + turn, self.counts[2])]
 
-    def greet(self):
+    def call(self):
         barrier = pltpu.get_barrier_semaphore()
         total = self.counts[2] - 1
         for dx, dy in AROUND:
@@ -76,7 +76,7 @@
             pl.semaphore_signal(
                 barrier, inc=1, device_id=tuple(self.peer(turn)), device_id_type=MESH_ID
             )
-        pl.semaphore_wait(barrier, total)
+        return barrier, total
 
 
 def opposite(step):
@@ -115,36 +115,54 @@
     return slice(margin, margin + size), slice(margin, margin + size)
 
 
-def spread_messages(place, brick, margins, ref, lanes, send, recv):
-    messages = []
-    for n, (dx, dy) in enumerate(AROUND):
-        from_x, to_x = edge_span(dx, brick[0], margins[0], HALO)
-        from_y, to_y = edge_span(dy, brick[1], margins[1], HALO)
-        messages.append(
-            Message(
-                place,
-                (dx, dy, 0),
-                ref.at[:, from_x, from_y, lanes],
-                ref.at[:, to_x, to_y, lanes],
-                send.at[n],
-                recv.at[n],
+def regions(brick, margins, reach):
+    found = []
+    for dx, dy in AROUND:
+        from_x, to_x = edge_span(dx, brick[0], margins[0], reach)
+        from_y, to_y = edge_span(dy, brick[1], margins[1], reach)
+        found.append(((dx, dy, 0), (from_x, from_y), (to_x, to_y)))
+    return sorted(found, key=lambda entry: (entry[0][1] == 0, entry[0][0] != 0))
+
+
+def spread_messages(place, brick, margins, ref, lanes, send, recv, reach):
+    return [
+        Message(
+            place,
+            step,
+            ref.at[:, source[0], source[1], lanes],
+            ref.at[:, target[0], target[1], lanes],
+            send.at[n],
+            recv.at[n],
+        )
+        for n, (step, source, target) in enumerate(regions(brick, margins, reach))
+    ]
+
+
+class Relay:
+    def __init__(self, place, step, ref, lanes, span, send, recv):
+        self.place, self.step = place, step
+        view = ref.at[:, span[0], span[1], lanes]
+        self.copies = [
+            pltpu.make_async_remote_copy(
+                src_ref=view,
+                dst_ref=view,
+                send_sem=send.at[turn - 1],
+                recv_sem=recv.at[turn - 1],
+                device_id=tuple(place.peer(turn)),
+                device_id_type=MESH_ID,
             )
-        )
-    return messages
-
-
-def peer_copies(place, ref, lanes, send, recv):
-    return [
-        pltpu.make_async_remote_copy(
-            src_ref=ref.at[:, :, :, lanes],
-            dst_ref=ref.at[:, :, :, lanes],
-            send_sem=send.at[turn - 1],
-            recv_sem=recv.at[turn - 1],
-            device_id=tuple(place.peer(turn)),
-            device_id_type=MESH_ID,
-        )
-        for turn in range(1, place.counts[2])
-    ]
+            for turn in range(1, place.counts[2])
+        ]
+
+    def when(self, action):
+        test = self.place.exists(self.step) if any(self.step) else None
+        action() if test is None else pl.when(test)(action)
+
+    def start(self):
+        self.when(lambda: [copy.start() for copy in self.copies] and None)
+
+    def wait(self):
+        self.when(lambda: [copy.wait() for copy in self.copies] and None)
 
 
 def clear_outside(place, brick, margins, refs, lanes):
@@ -156,33 +174,58 @@
         def _():
             for ref in refs:
                 for k in range(ref.shape[0]):
-                    shape = (to_x.stop - to_x.start, to_y.stop - to_y.start, brick[2])
+                    shape = (to_x.stop - to_x.start, to_y.stop - to_y.start, lanes.size)
                     ref[k, to_x, to_y, lanes] = jnp.zeros(shape, F32)
 
 
 def sweep_kernel(counts, brick, margins, forcing, start, modulus, zone_u, zone_w, *scratch):
     fields, rows_in, rows_out, sides = scratch[0:4], scratch[4], scratch[5], scratch[6:10]
     coupling, inverse = scratch[10:12]
-    face_send, face_recv, bulk_send, bulk_recv, peer_send, peer_recv = scratch[12:]
+    face_send, face_recv, bulk_send, bulk_recv, peer_send, peer_recv, load = scratch[12:]
     place = Place(counts)
     bx, by, bz = brick
     hx, hy = margins
     lanes = pl.ds(pl.multiple_of(place.here[2] * bz, bz), bz)
+    every = pl.ds(0, counts[2] * bz)
     row = iota((by, bz), 0)
     lane = iota((by, bz), 1)
+    own = (slice(hx, hx + bx), slice(hy, hy + by))
+    loads = [
+        pltpu.make_async_copy(start, fields[0].at[:3, 1 : bx + 1], load.at[0]),
+        pltpu.make_async_copy(modulus, fields[0].at[3, 1 : bx + 1], load.at[1]),
+        pltpu.make_async_copy(modulus, zone_w.at[3, own[0], own[1], lanes], load.at[2]),
+        pltpu.make_async_copy(forcing, zone_w.at[:3, own[0], own[1], lanes], load.at[3]),
+    ]
+    for copy in loads:
+        copy.start()
+    barrier, greetings = place.call()
+
+    clear_outside(place, brick, margins, (zone_u, zone_w), every)
+    for n, (dx, dy, dz) in enumerate(FACES):
+
+        @pl.when(jnp.logical_not(place.exists((dx, dy, dz))))
+        def _():
+            for sweep in range(FSWEEPS):
+                if dx:
+                    plane = 0 if dx < 0 else bx + 1
+                    for k in range(fields[sweep].shape[0]):
+                        fields[sweep][k, plane] = jnp.zeros((by, bz), F32)
+                elif dy:
+                    for k in range(4):
+                        rows_in[sweep, 0 if dy < 0 else 1, k] = jnp.zeros((bx, bz), F32)
+                else:
+                    for k in range(sides[sweep].shape[1]):
+                        blank = jnp.zeros((bx, by, bz), F32)
+                        sides[sweep][0 if dz < 0 else 1, k] = blank
+
+    loads[0].wait()
+    loads[1].wait()
 
     def stage(x, _):
-        for k in range(3):
-            u = start[k, x]
-            fields[0][k, x + 1] = u
+        for k in range(4):
+            u = fields[0][k, x + 1]
             rows_out[0, 0, k, pl.ds(x, 1), :] = u[:1]
             rows_out[0, 1, k, pl.ds(x, 1), :] = u[by - 1 :]
-            zone_w[k, hx + x, hy : hy + by, lanes] = forcing[k, x]
-        m = modulus[x]
-        fields[0][3, x + 1] = m
-        rows_out[0, 0, 3, pl.ds(x, 1), :] = m[:1]
-        rows_out[0, 1, 3, pl.ds(x, 1), :] = m[by - 1 :]
-        zone_w[3, hx + x, hy : hy + by, lanes] = m
         return 0
 
     lax.fori_loop(0, bx, stage, 0)
@@ -208,34 +251,37 @@
             )
         return messages
 
-    clear_outside(place, brick, margins, (zone_u, zone_w), lanes)
-    for n, (dx, dy, dz) in enumerate(FACES):
-
-        @pl.when(jnp.logical_not(place.exists((dx, dy, dz))))
-        def _():
-            for sweep in range(FSWEEPS):
-                if dx:
-                    plane = 0 if dx < 0 else bx + 1
-                    for k in range(fields[sweep].shape[0]):
-                        fields[sweep][k, plane] = jnp.zeros((by, bz), F32)
-                elif dy:
-                    for k in range(4):
-                        rows_in[sweep, 0 if dy < 0 else 1, k] = jnp.zeros((bx, bz), F32)
-                else:
-                    for k in range(sides[sweep].shape[1]):
-                        blank = jnp.zeros((bx, by, bz), F32)
-                        sides[sweep][0 if dz < 0 else 1, k] = blank
-
-    place.greet()
+    def relays(first, last, slot, ref, reach):
+        view = ref.at[first:last]
+        entries = [((0, 0, 0), own)]
+        entries += [(opposite(step), target) for step, _, target in regions(brick, margins, reach)]
+        return [
+            Relay(place, step, view, lanes, span, peer_send.at[slot, n], peer_recv.at[slot, n])
+            for n, (step, span) in enumerate(entries)
+        ]
+
+    pl.semaphore_wait(barrier, greetings)
     messages = faces(0)
     pending = list(messages)
     for message in messages:
         message.start()
-    bulk = spread_messages(
-        place, brick, margins, zone_w, lanes, bulk_send.at[0], bulk_recv.at[0]
-    )
-    for message in bulk:
-        message.start()
+    loads[2].wait()
+    loads[3].wait()
+    bulk, forward = [], []
+    for slot, (first, last, reach) in enumerate(((3, 4, HALO), (0, 1, HALO - 1), (1, 2, HALO - 1), (2, 3, HALO - 1))):
+        bulk.append(
+            spread_messages(
+                place,
+                brick,
+                margins,
+                zone_w.at[first:last],
+                lanes,
+                bulk_send.at[slot],
+                bulk_recv.at[slot],
+                reach,
+            )
+        )
+        forward.append(relays(first, last, slot, zone_w, reach))
 
     def around(sweep, k, x, u):
         low, high = rows_in[sweep, 0, k, pl.ds(x, 1), :], rows_in[sweep, 1, k, pl.ds(x, 1), :]
@@ -258,6 +304,9 @@
         return 0
 
     for sweep in range(FSWEEPS):
+        for message in bulk[sweep]:
+            message.start()
+        forward[sweep][0].start()
         for message in messages:
             message.arrived()
         if sweep == 0:
@@ -268,7 +317,7 @@
             scale = inverse[x]
             for k in range(3):
                 u = fields[sweep][k, x + 1]
-                total = forcing[k, x]
+                total = zone_w[k, hx + x, hy : hy + by, lanes]
                 for weight, other in zip(weights, around(sweep, k, x, u)):
                     total = total + weight * other
                 total = total * scale
@@ -286,25 +335,22 @@
             pending += messages
             for message in messages:
                 message.start()
-    last = spread_messages(
-        place, brick, margins, zone_u, lanes, bulk_send.at[1], bulk_recv.at[1]
+    final = spread_messages(
+        place, brick, margins, zone_u, lanes, bulk_send.at[4], bulk_recv.at[4], HALO
     )
-    for message in last:
+    for message in final:
         message.start()
-    for message in bulk:
-        message.arrived()
-    copies = peer_copies(place, zone_w, lanes, peer_send.at[0], peer_recv.at[0])
-    for copy in copies:
-        copy.start()
-    for message in last:
-        message.arrived()
-    more = peer_copies(place, zone_u, lanes, peer_send.at[1], peer_recv.at[1])
-    for copy in more:
-        copy.start()
-    for message in pending + bulk + last:
+    forward.append(relays(0, 3, 4, zone_u, HALO))
+    forward[4][0].start()
+    bulk.append(final)
+    for group, onward in zip(bulk, forward):
+        for message, relay in zip(group, onward[1:]):
+            message.arrived()
+            relay.start()
+    for message in pending + sum(bulk, []):
         message.sent()
-    for copy in copies + more:
-        copy.wait()
+    for relay in sum(forward, []):
+        relay.wait()
 
 
 def gather_kernel(counts, brick, margins, added, modulus, out, total, from_peer, *scratch):
@@ -326,11 +372,14 @@
         else:
             targets[n] = from_xy.at[dx + 1 + (dy + 1) // 2]
 
+    barrier, greetings = place.call()
+    for n, (dx, dy) in enumerate(AROUND):
+
         @pl.when(jnp.logical_not(place.exists((-dx, -dy, 0))))
         def _():
             targets[n][...] = jnp.zeros(targets[n].shape, F32)
 
-    place.greet()
+    pl.semaphore_wait(barrier, greetings)
     copies = [
         pltpu.make_async_remote_copy(
             src_ref=added.at[:, :, part(turn)],
@@ -357,8 +406,8 @@
     lax.fori_loop(0, total.shape[0], collect, 0)
     messages = []
     for n, (dx, dy) in enumerate(AROUND):
-        _, at_x = edge_span(-dx, bx, hx)
-        _, at_y = edge_span(-dy, by, hy)
+        _, at_x = edge_span(-dx, bx, hx, HALO - 1)
+        _, at_y = edge_span(-dy, by, hy, HALO - 1)
         messages.append(
             Message(place, (dx, dy, 0), total.at[at_x, at_y], targets[n], send.at[n], recv.at[n])
         )
@@ -373,8 +422,8 @@
     for message in messages:
         message.arrived()
     for n, (dx, dy) in enumerate(AROUND):
-        to_x, _ = edge_span(-dx, bx, hx)
-        to_y, _ = edge_span(-dy, by, hy)
+        to_x, _ = edge_span(-dx, bx, hx, HALO - 1)
+        to_y, _ = edge_span(-dy, by, hy, HALO - 1)
         out[to_x.start - hx : to_x.stop - hx, to_y.start - hy : to_y.stop - hy, :] += targets[n][...]
     for message in messages:
         message.sent()
@@ -691,7 +740,7 @@
     shift = lax.rem(whole_lanes - begin[2], whole_lanes)
     shift_y = lax.rem(whole_rows - begin[1], whole_rows)
     z = begin[2] + iota((rows, 128), 1)
-    inside = (z >= 0) & (z < depth)
+    inside = (z >= 0) & (z < depth) & (iota((rows, 128), 0) < count)
 
     def cut(x, _):
         def take(ref, k):
@@ -707,16 +756,21 @@
     lax.fori_loop(0, count, cut, 0)
 
 
-def zone_kernel(counts, brick, margins, corners, zone_all_u, zone_all_w, field_out, added, *scratch):
+def zone_kernel(counts, brick, margins, where, zone_all_u, zone_all_w, field_out, added, *scratch):
+    scratch, (corners, ready) = scratch[:-2], scratch[-2:]
     zone_u, zone_f, zone_m = scratch[:3]
     temp, fields, packed, flat, bands, slopes, mat, side, lowers, solved, spread = scratch[3:]
     bx, by, bz = brick
     hx, hy = margins
     here = [lax.axis_index(name) for name in AXES]
     lanes = pl.ds(pl.multiple_of(here[2] * bz, bz), bz)
-    for k in range(3):
-        field_out[k] = zone_all_u[k, hx : hx + bx, hy : hy + by, lanes]
+    fetch = pltpu.make_async_copy(where, corners, ready.at[0])
+    fetch.start()
+    inner = zone_all_u.at[:, hx : hx + bx, hy : hy + by, lanes]
+    store = pltpu.make_async_copy(inner, field_out, ready.at[1])
+    store.start()
     added[...] = jnp.zeros_like(added)
+    fetch.wait()
     for number in range(corners.shape[0]):
         begin = [
             corners[number, 0] - here[0] * bx + hx - 1,
@@ -731,6 +785,7 @@
         assemble(bands, slopes, mat, side)
         solve_zone(fields.shape[1], mat, side, lowers, solved, spread)
         place_zone(begin, zone_m, spread, temp, added)
+    store.wait()
 
 
 def body(forcing, start_field, modulus, corners):
@@ -748,7 +803,7 @@
             jax.ShapeDtypeStruct((3, *span), F32),
             jax.ShapeDtypeStruct((4, *span), F32),
         ),
-        in_specs=[whole, whole, whole],
+        in_specs=[pl.BlockSpec(memory_space=pltpu.HBM)] * 3,
         out_specs=(whole, whole),
         scratch_shapes=[
             pltpu.VMEM((4, bx + 2, by, bz), F32),
@@ -761,16 +816,17 @@
             pltpu.VMEM((bx, by, bz), F32),
             dma((FSWEEPS, len(FACES))),
             dma((FSWEEPS, len(FACES))),
-            dma((2, len(AROUND))),
-            dma((2, len(AROUND))),
-            dma((2, peers)),
-            dma((2, peers)),
+            dma((5, len(AROUND))),
+            dma((5, len(AROUND))),
+            dma((5, len(AROUND) + 1, peers)),
+            dma((5, len(AROUND) + 1, peers)),
+            dma((4,)),
         ],
         compiler_params=pltpu.CompilerParams(
             collective_id=0, has_side_effects=True, vmem_limit_bytes=40 * 1024 * 1024
         ),
         name="sweeps",
-    )(forcing, start_field, modulus)
+    )(*[pltpu.with_memory_space_constraint(each, pltpu.HBM) for each in (forcing, start_field, modulus)])
     zone_span = 2 * PC + 2
     zone_rows = -(-zone_span // 8) * 8
     size = -(-PC * PC // 8) * 8
@@ -781,8 +837,8 @@
             jax.ShapeDtypeStruct(forcing.shape, F32),
             jax.ShapeDtypeStruct(tuple(span), F32),
         ),
-        in_specs=[pl.BlockSpec(memory_space=pltpu.SMEM), whole, whole],
-        out_specs=(whole, whole),
+        in_specs=[pl.BlockSpec(memory_space=pltpu.HBM), whole, whole],
+        out_specs=(pl.BlockSpec(memory_space=pl.ANY), whole),
         scratch_shapes=[
             pltpu.VMEM((3, zone_span, zone_rows, 128), F32),
             pltpu.VMEM((3, zone_span, zone_rows, 128), F32),
@@ -798,10 +854,12 @@
             pltpu.VMEM((2, planes, 128, 128), F32),
             pltpu.VMEM((2, planes, 128, 256), F32),
             pltpu.VMEM((128, 128), F32),
+            pltpu.SMEM(corners.shape, jnp.int32),
+            dma((2,)),
         ],
         compiler_params=pltpu.CompilerParams(vmem_limit_bytes=40 * 1024 * 1024),
         name="zone",
-    )(corners, zone_all_u, zone_all_w)
+    )(pltpu.with_memory_space_constraint(corners, pltpu.HBM), zone_all_u, zone_all_w)
     updated = pl.pallas_call(
         functools.partial(gather_kernel, counts, brick, margins),
         out_shape=jax.ShapeDtypeStruct(brick, F32),
@@ -810,9 +868,9 @@
         scratch_shapes=[
             pltpu.VMEM((span[0], span[1], bz), F32),
             pltpu.VMEM((peers, span[0], span[1], bz), F32),
-            pltpu.VMEM((2, margins[0], by, bz), F32),
-            pltpu.VMEM((2, bx, margins[1], bz), F32),
-            pltpu.VMEM((4, margins[0], margins[1], bz), F32),
+            pltpu.VMEM((2, HALO - 1, by, bz), F32),
+            pltpu.VMEM((2, bx, HALO - 1, bz), F32),
+            pltpu.VMEM((4, HALO - 1, HALO - 1, bz), F32),
             dma((len(AROUND),)),
             dma((len(AROUND),)),
             dma((peers,)),

time: 110 us -> 97.3 us (0.88); the launches traced: 108 us -> 97.2 us
  Pallas kernels: 103 us -> 95.9 us
  local copies, waits for them, and re-layouts: 4.2 us -> 0.66 us
    pallas_call x1, Pallas kernels: 45.9 us -> 38.2 us  [body(): pl.pallas_call(functools.partial(sweep_kernel, counts, brick, margins), o...]
    unnamed x9 -> x3, local copies, waits for them, and re-layouts: 4.2 us -> 0.66 us
where the time goes in v3:
time: 97.3 us; the launch traced here: 97.2 us
  Pallas kernels  95.9 us (99%)
    pallas_call x1, Pallas kernels, body(): pl.pallas_call(functools.partial(zone_kernel, counts, brick, margins), ou...  44.4 us
    pallas_call x1, Pallas kernels, body(): pl.pallas_call(functools.partial(sweep_kernel, counts, brick, margins), o...  38.2 us
    pallas_call x1, Pallas kernels, body(): pl.pallas_call(functools.partial(gather_kernel, counts, brick, margins),...  13.2 us

profile of v3, /device:TPU:0, one launch (start us, length us, event | category | flops | bytes accessed | tf_op | source)
XLA Modules:
  0.0 97.2 jit_solution(15059030043766029350)
XLA Ops:
  0.6 0.0 copy-start
  0.6 38.2 %sweeps.1 = (f32[3,28,32,256]{3,2,1,0:T(8,128)S(1)}, f32[4,28,32,256]{3,2,1,0:T(8,128)S(1)}) custom-call(f32[3,16,16,128]{3,2,1,0:T(8,128)} %forcing.1, f32[3,16,16,128]{3,2,1,0:T(8,128)} %start.1, f32[16,16,128]{2,1,0:T(8,128)} %modulus.3), custom_call_target="tpu_custom_call" | custom-call | tf_op jit(solution)/shard_map/sweeps/pallas_call | solution.py:800
  38.9 44.4 %zone.1 = (f32[3,16,16,128]{3,2,1,0:T(8,128)}, f32[28,32,256]{2,1,0:T(8,128)S(1)}) custom-call(s32[1,3]{1,0:T(1,128)} %where.1, f32[3,28,32,256]{3,2,1,0:T(8,128)S(1)} %get-tuple-element.6.zone_all_u, f32[4,28,32,256]{3,2,1,0:T(8,128)S(1)} %get-tuple-element.7.zone_all_w), custom_call_target="tpu_custom_call" | custom-call | tf_op jit(solution)/shard_map/zone/pallas_call | solution.py:834
  83.3 0.0 copy-done
  83.3 13.2 %gather.1 = f32[16,16,128]{2,1,0:T(8,128)S(1)} custom-call(f32[28,32,256]{2,1,0:T(8,128)S(1)} %get-tuple-element.9.added, f32[16,16,128]{2,1,0:T(8,128)S(1)} %copy-done), custom_call_target="tpu_custom_call" | custom-call | tf_op jit(solution)/shard_map/gather/pallas_call | solution.py:863
  96.5 0.7 copy.7
Async XLA Ops:
  0.6 82.7 %copy-start = (f32[16,16,128]{2,1,0:T(8,128)S(1)}, f32[16,16,128]{2,1,0:T(8,128)}, u32[]{:S(2)}) copy-start(f32[16,16,128]{2,1,0:T(8,128)} %modulus.3) | copy-start | bytes 393220

commit v4 on v3

--- a/solution.py
+++ b/solution.py
@@ -20,9 +20,9 @@
 F32 = jnp.float32
 
 
-def dot(a, b, contract):
+def dot(a, b, contract, precision=lax.Precision.HIGH):
     return lax.dot_general(
-        a, b, ((contract[:1], contract[1:]), ((), ())), precision=HIGHEST, preferred_element_type=F32
+        a, b, ((contract[:1], contract[1:]), ((), ())), precision=precision, preferred_element_type=F32
     )
 
 
@@ -230,22 +230,21 @@
 
     lax.fori_loop(0, bx, stage, 0)
 
-    def faces(sweep):
-        channels = 4 if sweep == 0 else 3
+    def faces(sweep, k):
         field = fields[sweep]
         messages = []
         for n, step in enumerate(FACES):
             dx, dy, dz = step
             if dx:
-                source = field.at[:, bx if dx > 0 else 1]
-                target = field.at[:, 0 if dx > 0 else bx + 1]
+                source = field.at[k, bx if dx > 0 else 1]
+                target = field.at[k, 0 if dx > 0 else bx + 1]
             elif dy:
-                source = rows_out.at[sweep, 1 if dy > 0 else 0, :channels]
-                target = rows_in.at[sweep, 0 if dy > 0 else 1, :channels]
+                source = rows_out.at[sweep, 1 if dy > 0 else 0, k]
+                target = rows_in.at[sweep, 0 if dy > 0 else 1, k]
             else:
-                source = field.at[:, 1 : bx + 1]
-                target = sides[sweep].at[0 if dz > 0 else 1]
-            at = (sweep, n)
+                source = field.at[k, 1 : bx + 1]
+                target = sides[sweep].at[0 if dz > 0 else 1, k]
+            at = (sweep, k, n)
             messages.append(
                 Message(place, step, source, target, face_send.at[at], face_recv.at[at])
             )
@@ -261,9 +260,9 @@
         ]
 
     pl.semaphore_wait(barrier, greetings)
-    messages = faces(0)
-    pending = list(messages)
-    for message in messages:
+    waiting = {(0, k): faces(0, k) for k in (3, 0, 1, 2)}
+    pending = sum(waiting.values(), [])
+    for message in pending:
         message.start()
     loads[2].wait()
     loads[3].wait()
@@ -307,42 +306,51 @@
         for message in bulk[sweep]:
             message.start()
         forward[sweep][0].start()
-        for message in messages:
-            message.arrived()
         if sweep == 0:
+            for message in waiting[0, 3]:
+                message.arrived()
             lax.fori_loop(0, bx, couple, 0)
-
-        def relax(x, _, sweep=sweep):
-            weights = [coupling[n, x] for n in range(6)]
-            scale = inverse[x]
-            for k in range(3):
+        for k in range(3):
+            for message in waiting[sweep, k]:
+                message.arrived()
+
+            def relax(x, _, sweep=sweep, k=k):
                 u = fields[sweep][k, x + 1]
                 total = zone_w[k, hx + x, hy : hy + by, lanes]
-                for weight, other in zip(weights, around(sweep, k, x, u)):
-                    total = total + weight * other
-                total = total * scale
+                for n, other in enumerate(around(sweep, k, x, u)):
+                    total = total + coupling[n, x] * other
+                total = total * inverse[x]
                 if sweep < FSWEEPS - 1:
                     fields[sweep + 1][k, x + 1] = total
                     rows_out[sweep + 1, 0, k, pl.ds(x, 1), :] = total[:1]
                     rows_out[sweep + 1, 1, k, pl.ds(x, 1), :] = total[by - 1 :]
                 else:
                     zone_u[k, hx + x, hy : hy + by, lanes] = total
-            return 0
-
-        lax.fori_loop(0, bx, relax, 0)
-        if sweep < FSWEEPS - 1:
-            messages = faces(sweep + 1)
-            pending += messages
-            for message in messages:
-                message.start()
-    final = spread_messages(
-        place, brick, margins, zone_u, lanes, bulk_send.at[4], bulk_recv.at[4], HALO
-    )
-    for message in final:
-        message.start()
-    forward.append(relays(0, 3, 4, zone_u, HALO))
-    forward[4][0].start()
-    bulk.append(final)
+                return 0
+
+            lax.fori_loop(0, bx, relax, 0)
+            if sweep < FSWEEPS - 1:
+                waiting[sweep + 1, k] = faces(sweep + 1, k)
+                pending += waiting[sweep + 1, k]
+                for message in waiting[sweep + 1, k]:
+                    message.start()
+            else:
+                slot = FSWEEPS + k
+                final = spread_messages(
+                    place,
+                    brick,
+                    margins,
+                    zone_u.at[k : k + 1],
+                    lanes,
+                    bulk_send.at[slot],
+                    bulk_recv.at[slot],
+                    HALO,
+                )
+                for message in final:
+                    message.start()
+                bulk.append(final)
+                forward.append(relays(k, k + 1, slot, zone_u, HALO))
+                forward[slot][0].start()
     for group, onward in zip(bulk, forward):
         for message, relay in zip(group, onward[1:]):
             message.arrived()
@@ -601,10 +609,14 @@
     fill(0, meet + 1, meet + 1, bands, slopes, mat, side, 0)
 
 
+GROUPS = 5
+
+
 def factored(blocks, count):
     lane = iota((8, 128), 1)
     sub = iota((8, 128), 0)
     tiles = -(-count // 8)
+    chains = range(len(blocks))
 
     def over_lanes(value, at):
         return jnp.broadcast_to(value[:, at : at + 1], value.shape)
@@ -615,37 +627,66 @@
     grids = [[block[8 * q : 8 * q + 8] for q in range(tiles)] for block in blocks]
     lower = [[] for _ in blocks]
     scaled = [[] for _ in blocks]
-    for p in range(tiles):
-        pivots = range(8 * p, min(8 * p + 8, count))
-        within = (lane >= pivots[0]) & (lane <= pivots[-1])
-        keep = (lane <= pivots[-1]) & (sub < len(pivots))
-        for grid, low, high in zip(grids, lower, scaled):
-            panel = grid[p]
+    first = 0
+    while first < tiles:
+        last = min(first + GROUPS, tiles)
+        for p in range(first, last):
+            width = min(8, count - 8 * p)
+            within = (lane >= 8 * p) & (lane < 8 * p + width)
             unit = jnp.where(lane - 8 * p == sub, 1.0, 0.0)
-            low.append(jnp.where(keep, jnp.where(within, unit, panel), 0.0))
-            columns = [over_lanes(panel, j) for j in pivots]
-            for i, j in enumerate(pivots):
-                column = columns[i]
-                pivot = 1.0 / over_rows(column, i)
-                row = jnp.where(lane == j, pivot, over_rows(panel, i) * pivot)
-                for n in range(i + 1, len(pivots)):
-                    crossing = over_rows(columns[n], i) * pivot
-                    columns[n] = jnp.where(sub == i, crossing, columns[n] - column * crossing)
-                cleared = jnp.where(lane == j, 0.0, panel)
-                panel = jnp.where(sub == i, row, cleared - column * row)
-            high.append(jnp.where(keep, panel, 0.0))
-            rows = [over_rows(panel, i) for i in range(len(pivots))]
-            for q in range(p + 1, tiles):
-                old = grid[q]
-                terms = [over_lanes(old, j) * row for j, row in zip(pivots, rows)]
-                while len(terms) > 1:
-                    pairs = [terms[n] + terms[n + 1] for n in range(0, len(terms) - 1, 2)]
-                    terms = pairs + terms[len(terms) - len(terms) % 2 :]
-                grid[q] = jnp.where(within, 0.0, old) - terms[0]
-    return [
-        (jnp.concatenate(low, axis=0), jnp.concatenate(high, axis=0))
-        for low, high in zip(lower, scaled)
-    ]
+            for c in chains:
+                grid = grids[c]
+                panel = grid[p]
+                columns = [over_lanes(panel, 8 * p + n) for n in range(width)]
+                panel = jnp.where(within, unit, panel)
+                lower[c].append(panel)
+                rows = [over_rows(panel, n) for n in range(width)]
+                for i in range(width):
+                    j = 8 * p + i
+                    column = columns[i]
+                    pivot = 1.0 / over_rows(column, i)
+                    row = over_rows(panel, i) * pivot
+                    for n in range(i + 1, width):
+                        crossing = over_rows(columns[n], i) * pivot
+                        columns[n] = jnp.where(sub == i, crossing, columns[n] - column * crossing)
+                    panel = jnp.where(sub == i, row, panel - column * row)
+                rows = [over_rows(panel, n) for n in range(width)]
+                panel = rows[0]
+                for n in range(1, width):
+                    panel = jnp.where(sub == n, rows[n], panel)
+                scaled[c].append(panel)
+                for q in range(p + 1, last):
+                    old = grid[q]
+                    terms = [over_lanes(old, 8 * p + n) * row for n, row in enumerate(rows)]
+                    while len(terms) > 1:
+                        pairs = [terms[n] + terms[n + 1] for n in range(0, len(terms) - 1, 2)]
+                        terms = pairs + terms[len(terms) - len(terms) % 2 :]
+                    grid[q] = jnp.where(within, 0.0, old) - terms[0]
+        if last < tiles:
+            within = (lane >= 8 * first) & (lane < 8 * last)
+            for c in chains:
+                low = jnp.concatenate(lower[c][first:last], axis=0)
+                high = jnp.concatenate(
+                    [
+                        jnp.where((lane < 8 * p + 8) | (lane >= 8 * last), scaled[c][p], 0.0)
+                        for p in range(first, last)
+                    ],
+                    axis=0,
+                )
+                change = dot(low, high, (0, 0))
+                for q in range(last, tiles):
+                    old = jnp.where(within, 0.0, grids[c][q])
+                    grids[c][q] = old - change[8 * q : 8 * q + 8]
+        first = last
+
+    def trimmed(parts):
+        kept = []
+        for p, part in enumerate(parts):
+            limit = min(8 * p + 8, count)
+            kept.append(jnp.where((lane < limit) & (sub < limit - 8 * p), part, 0.0))
+        return jnp.concatenate(kept, axis=0)
+
+    return [(trimmed(lower[c]), trimmed(scaled[c])) for c in chains]
 
 
 def eliminate(t, chains, size, mat, side, lowers, solved, more=True):
@@ -672,8 +713,8 @@
     params = PC * PC
     meet = PC // 2 - 1
     mark = iota((128, 128), 1) == params
-    lowers[...] = jnp.zeros_like(lowers)
-    solved[...] = jnp.zeros_like(solved)
+    for ref in (lowers, solved):
+        ref[:, :, size:, :] = jnp.zeros((*ref.shape[:2], ref.shape[2] - size, ref.shape[3]), F32)
 
     def both(t, _):
         eliminate(t, (0, 1), size, mat, side, lowers, solved)
@@ -814,12 +855,12 @@
             *[pltpu.VMEM((2, 3, bx, by, bz), F32)] * (FSWEEPS - 1),
             pltpu.VMEM((6, bx, by, bz), F32),
             pltpu.VMEM((bx, by, bz), F32),
-            dma((FSWEEPS, len(FACES))),
-            dma((FSWEEPS, len(FACES))),
-            dma((5, len(AROUND))),
-            dma((5, len(AROUND))),
-            dma((5, len(AROUND) + 1, peers)),
-            dma((5, len(AROUND) + 1, peers)),
+            dma((FSWEEPS, 4, len(FACES))),
+            dma((FSWEEPS, 4, len(FACES))),
+            dma((FSWEEPS + 3, len(AROUND))),
+            dma((FSWEEPS + 3, len(AROUND))),
+            dma((FSWEEPS + 3, len(AROUND) + 1, peers)),
+            dma((FSWEEPS + 3, len(AROUND) + 1, peers)),
             dma((4,)),
         ],
         compiler_params=pltpu.CompilerParams(

time: 97.3 us -> 88.7 us (0.912)
  Pallas kernels: 95.9 us -> 87.2 us
    pallas_call x1, Pallas kernels: 44.4 us -> 36.6 us  [body(): pl.pallas_call(functools.partial(zone_kernel, counts, brick, margins), ou...]
    pallas_call x1, Pallas kernels: 13.2 us -> 11.5 us  [body(): pl.pallas_call(functools.partial(gather_kernel, counts, brick, margins),...]
where the time goes in v4:
time: 88.7 us; the launch traced here: 88.5 us
  Pallas kernels  87.2 us (98%)
    pallas_call x1, Pallas kernels, body(): pl.pallas_call(functools.partial(sweep_kernel, counts, brick, margins), o...  39.1 us
    pallas_call x1, Pallas kernels, body(): pl.pallas_call(functools.partial(zone_kernel, counts, brick, margins), ou...  36.6 us
    pallas_call x1, Pallas kernels, body(): pl.pallas_call(functools.partial(gather_kernel, counts, brick, margins),...  11.5 us

profile of v4, /device:TPU:0, one launch (start us, length us, event | category | flops | bytes accessed | tf_op | source)
XLA Modules:
  0.0 88.5 jit_solution(9955724302880195639)
XLA Ops:
  0.6 0.0 copy-start
  0.6 39.1 %sweeps.1 = (f32[3,28,32,256]{3,2,1,0:T(8,128)S(1)}, f32[4,28,32,256]{3,2,1,0:T(8,128)S(1)}) custom-call(f32[3,16,16,128]{3,2,1,0:T(8,128)} %forcing.1, f32[3,16,16,128]{3,2,1,0:T(8,128)} %start.1, f32[16,16,128]{2,1,0:T(8,128)} %modulus.3), custom_call_target="tpu_custom_call" | custom-call | tf_op jit(solution)/shard_map/sweeps/pallas_call | solution.py:841
  39.7 36.6 %zone.1 = (f32[3,16,16,128]{3,2,1,0:T(8,128)}, f32[28,32,256]{2,1,0:T(8,128)S(1)}) custom-call(s32[1,3]{1,0:T(1,128)} %where.1, f32[3,28,32,256]{3,2,1,0:T(8,128)S(1)} %get-tuple-element.6.zone_all_u, f32[4,28,32,256]{3,2,1,0:T(8,128)S(1)} %get-tuple-element.7.zone_all_w), custom_call_target="tpu_custom_call" | custom-call | tf_op jit(solution)/shard_map/zone/pallas_call | solution.py:875
  76.4 0.0 copy-done
  76.4 11.5 %gather.1 = f32[16,16,128]{2,1,0:T(8,128)S(1)} custom-call(f32[28,32,256]{2,1,0:T(8,128)S(1)} %get-tuple-element.9.added, f32[16,16,128]{2,1,0:T(8,128)S(1)} %copy-done), custom_call_target="tpu_custom_call" | custom-call | tf_op jit(solution)/shard_map/gather/pallas_call | solution.py:904
  87.9 0.7 copy.7
Async XLA Ops:
  0.6 75.7 %copy-start = (f32[16,16,128]{2,1,0:T(8,128)S(1)}, f32[16,16,128]{2,1,0:T(8,128)}, u32[]{:S(2)}) copy-start(f32[16,16,128]{2,1,0:T(8,128)} %modulus.3) | copy-start | bytes 393220

commit v5 on v4

--- a/solution.py
+++ b/solution.py
@@ -121,7 +121,7 @@
         from_x, to_x = edge_span(dx, brick[0], margins[0], reach)
         from_y, to_y = edge_span(dy, brick[1], margins[1], reach)
         found.append(((dx, dy, 0), (from_x, from_y), (to_x, to_y)))
-    return sorted(found, key=lambda entry: (entry[0][1] == 0, entry[0][0] != 0))
+    return sorted(found, key=lambda entry: (entry[0][1] == 0, entry[0][0] == 0))
 
 
 def spread_messages(place, brick, margins, ref, lanes, send, recv, reach):
@@ -200,7 +200,6 @@
         copy.start()
     barrier, greetings = place.call()
 
-    clear_outside(place, brick, margins, (zone_u, zone_w), every)
     for n, (dx, dy, dz) in enumerate(FACES):
 
         @pl.when(jnp.logical_not(place.exists((dx, dy, dz))))
@@ -307,6 +306,7 @@
             message.start()
         forward[sweep][0].start()
         if sweep == 0:
+            clear_outside(place, brick, margins, (zone_u, zone_w), every)
             for message in waiting[0, 3]:
                 message.arrived()
             lax.fori_loop(0, bx, couple, 0)
@@ -448,7 +448,19 @@
     first_z = iota((rows, 128), 1) % 2 == 1
     rank = iota((PC, 128), 0)
     lane = iota((PC, 128), 1)
+    steps = ((0, 1), (0, -1), (1, 1), (1, -1), (2, 1), (2, -1))
     for x in range(PC):
+        middles, others = [], []
+        for a in range(2):
+            at = 2 * x + 1 + a
+            m = zone_m[at]
+            middles.append(m)
+            others.append(
+                [
+                    zone_m[at + step] if axis == 0 else roll(m, -step, axis - 1)
+                    for axis, step in steps
+                ]
+            )
         for k in range(3):
             sums = [None] * FIELDS
 
@@ -457,16 +469,12 @@
 
             for a in range(2):
                 at = 2 * x + 1 + a
-                u, m = zone_u[k, at], zone_m[at]
+                u, m = zone_u[k, at], middles[a]
                 applied = MASS_TERM * u
                 laplace = jnp.zeros_like(u)
-                for number, (axis, step) in enumerate(
-                    ((0, 1), (0, -1), (1, 1), (1, -1), (2, 1), (2, -1))
-                ):
-                    if axis == 0:
-                        u_next, m_next = zone_u[k, at + step], zone_m[at + step]
-                    else:
-                        u_next, m_next = roll(u, -step, axis - 1), roll(m, -step, axis - 1)
+                for number, (axis, step) in enumerate(steps):
+                    u_next = zone_u[k, at + step] if axis == 0 else roll(u, -step, axis - 1)
+                    m_next = others[a][number]
                     change = u - u_next
                     applied = applied + 0.5 * (m + m_next) * change
                     laplace = laplace + change
@@ -596,8 +604,10 @@
 
 def assemble(bands, slopes, mat, side):
     meet = PC // 2 - 1
-    mat[...] = jnp.zeros_like(mat)
-    side[...] = jnp.zeros_like(side)
+    for at in (meet, meet + 1):
+        mat[1, at] = jnp.zeros(mat.shape[2:], F32)
+        for c in range(2):
+            side[c, at] = jnp.zeros(side.shape[2:], F32)
 
     def both(t, _):
         fill(0, t, t, bands, slopes, mat, side, 2)
@@ -778,8 +788,8 @@
 def cut_zone(begin, depth, zone_all_u, zone_all_w, zone_u, zone_f, zone_m):
     count, rows = zone_m.shape[:2]
     whole_rows, whole_lanes = zone_all_u.shape[-2:]
+    shift_y = lax.rem(whole_rows - begin[1], whole_rows)
     shift = lax.rem(whole_lanes - begin[2], whole_lanes)
-    shift_y = lax.rem(whole_rows - begin[1], whole_rows)
     z = begin[2] + iota((rows, 128), 1)
     inside = (z >= 0) & (z < depth) & (iota((rows, 128), 0) < count)
 
@@ -819,7 +829,8 @@
             corners[number, 2] - 1,
         ]
         cut_zone(begin, counts[2] * bz, zone_all_u, zone_all_w, zone_u, zone_f, zone_m)
-        fields[...] = jnp.zeros_like(fields)
+        rest = fields.shape[1] - PC * PC
+        fields[:, PC * PC :, :] = jnp.zeros((fields.shape[0], rest, 128), F32)
         coarse_fields(zone_u, zone_f, zone_m, temp, fields)
         transpose_fields(fields, packed, flat)
         band_sums(flat, packed, bands, slopes)

time: 88.7 us -> 88.2 us (level)
  no operation moved by 1% of the time
where the time goes in v5:
time: 88.2 us; the launch traced here: 88.1 us
  Pallas kernels  86.7 us (98%)
    pallas_call x1, Pallas kernels, body(): pl.pallas_call(functools.partial(sweep_kernel, counts, brick, margins), o...  39 us
    pallas_call x1, Pallas kernels, body(): pl.pallas_call(functools.partial(zone_kernel, counts, brick, margins), ou...  36.3 us
    pallas_call x1, Pallas kernels, body(): pl.pallas_call(functools.partial(gather_kernel, counts, brick, margins),...  11.4 us

profile of v5, /device:TPU:0, one launch (start us, length us, event | category | flops | bytes accessed | tf_op | source)
XLA Modules:
  0.0 88.1 jit_solution(3149644220708401208)
XLA Ops:
  0.6 0.0 copy-start
  0.6 39.0 %sweeps.1 = (f32[3,28,32,256]{3,2,1,0:T(8,128)S(1)}, f32[4,28,32,256]{3,2,1,0:T(8,128)S(1)}) custom-call(f32[3,16,16,128]{3,2,1,0:T(8,128)} %forcing.1, f32[3,16,16,128]{3,2,1,0:T(8,128)} %start.1, f32[16,16,128]{2,1,0:T(8,128)} %modulus.3), custom_call_target="tpu_custom_call" | custom-call | tf_op jit(solution)/shard_map/sweeps/pallas_call | solution.py:852
  39.7 36.3 %zone.1 = (f32[3,16,16,128]{3,2,1,0:T(8,128)}, f32[28,32,256]{2,1,0:T(8,128)S(1)}) custom-call(s32[1,3]{1,0:T(1,128)} %where.1, f32[3,28,32,256]{3,2,1,0:T(8,128)S(1)} %get-tuple-element.6.zone_all_u, f32[4,28,32,256]{3,2,1,0:T(8,128)S(1)} %get-tuple-element.7.zone_all_w), custom_call_target="tpu_custom_call" | custom-call | tf_op jit(solution)/shard_map/zone/pallas_call | solution.py:886
  76.0 0.0 copy-done
  76.0 11.4 %gather.1 = f32[16,16,128]{2,1,0:T(8,128)S(1)} custom-call(f32[28,32,256]{2,1,0:T(8,128)S(1)} %get-tuple-element.9.added, f32[16,16,128]{2,1,0:T(8,128)S(1)} %copy-done), custom_call_target="tpu_custom_call" | custom-call | tf_op jit(solution)/shard_map/gather/pallas_call | solution.py:915
  87.4 0.7 copy.7
Async XLA Ops:
  0.6 75.4 %copy-start = (f32[16,16,128]{2,1,0:T(8,128)S(1)}, f32[16,16,128]{2,1,0:T(8,128)}, u32[]{:S(2)}) copy-start(f32[16,16,128]{2,1,0:T(8,128)} %modulus.3) | copy-start | bytes 393220

commit v6 on v5

--- a/solution.py
+++ b/solution.py
@@ -38,6 +38,18 @@
 AXES = ("gx", "gy", "gz")
 AROUND = tuple((dx, dy) for dx in (-1, 0, 1) for dy in (-1, 0, 1) if (dx, dy) != (0, 0))
 FACES = ((-1, 0, 0), (1, 0, 0), (0, -1, 0), (0, 1, 0), (0, 0, -1), (0, 0, 1))
+
+
+def each(count, step, width):
+    while count % width:
+        width -= 1
+
+    def several(n, _):
+        for i in range(width):
+            step(width * n + i, 0)
+        return 0
+
+    lax.fori_loop(0, count // width, several, 0)
 
 
 class Place:
@@ -227,7 +239,7 @@
             rows_out[0, 1, k, pl.ds(x, 1), :] = u[by - 1 :]
         return 0
 
-    lax.fori_loop(0, bx, stage, 0)
+    each(bx, stage, 4)
 
     def faces(sweep, k):
         field = fields[sweep]
@@ -309,7 +321,7 @@
             clear_outside(place, brick, margins, (zone_u, zone_w), every)
             for message in waiting[0, 3]:
                 message.arrived()
-            lax.fori_loop(0, bx, couple, 0)
+            each(bx, couple, 2)
         for k in range(3):
             for message in waiting[sweep, k]:
                 message.arrived()
@@ -328,7 +340,7 @@
                     zone_u[k, hx + x, hy : hy + by, lanes] = total
                 return 0
 
-            lax.fori_loop(0, bx, relax, 0)
+            each(bx, relax, 4)
             if sweep < FSWEEPS - 1:
                 waiting[sweep + 1, k] = faces(sweep + 1, k)
                 pending += waiting[sweep + 1, k]
@@ -804,7 +816,7 @@
         zone_m[x] = take(zone_all_w, 3)
         return 0
 
-    lax.fori_loop(0, count, cut, 0)
+    each(count, cut, 2)
 
 
 def zone_kernel(counts, brick, margins, where, zone_all_u, zone_all_w, field_out, added, *scratch):

time: 88.2 us -> 84.3 us (0.956)
  Pallas kernels: 86.7 us -> 82.8 us
    pallas_call x1, Pallas kernels: 39 us -> 35.3 us  [body(): pl.pallas_call(functools.partial(sweep_kernel, counts, brick, margins), o...]
where the time goes in v6:
time: 84.3 us; the launch traced here: 84.1 us
  Pallas kernels  82.8 us (98%)
    pallas_call x1, Pallas kernels, body(): pl.pallas_call(functools.partial(zone_kernel, counts, brick, margins), ou...  35.5 us
    pallas_call x1, Pallas kernels, body(): pl.pallas_call(functools.partial(sweep_kernel, counts, brick, margins), o...  35.3 us
    pallas_call x1, Pallas kernels, body(): pl.pallas_call(functools.partial(gather_kernel, counts, brick, margins),...  11.9 us

profile of v6, /device:TPU:0, one launch (start us, length us, event | category | flops | bytes accessed | tf_op | source)
XLA Modules:
  0.0 84.1 jit_solution(17179134457500193115)
XLA Ops:
  0.6 0.0 copy-start
  0.6 35.3 %sweeps.1 = (f32[3,28,32,256]{3,2,1,0:T(8,128)S(1)}, f32[4,28,32,256]{3,2,1,0:T(8,128)S(1)}) custom-call(f32[3,16,16,128]{3,2,1,0:T(8,128)} %forcing.1, f32[3,16,16,128]{3,2,1,0:T(8,128)} %start.1, f32[16,16,128]{2,1,0:T(8,128)} %modulus.3), custom_call_target="tpu_custom_call" | custom-call | tf_op jit(solution)/shard_map/sweeps/pallas_call | solution.py:864
  35.9 35.5 %zone.1 = (f32[3,16,16,128]{3,2,1,0:T(8,128)}, f32[28,32,256]{2,1,0:T(8,128)S(1)}) custom-call(s32[1,3]{1,0:T(1,128)} %where.1, f32[3,28,32,256]{3,2,1,0:T(8,128)S(1)} %get-tuple-element.6.zone_all_u, f32[4,28,32,256]{3,2,1,0:T(8,128)S(1)} %get-tuple-element.7.zone_all_w), custom_call_target="tpu_custom_call" | custom-call | tf_op jit(solution)/shard_map/zone/pallas_call | solution.py:898
  71.5 0.0 copy-done
  71.5 11.9 %gather.1 = f32[16,16,128]{2,1,0:T(8,128)S(1)} custom-call(f32[28,32,256]{2,1,0:T(8,128)S(1)} %get-tuple-element.9.added, f32[16,16,128]{2,1,0:T(8,128)S(1)} %copy-done), custom_call_target="tpu_custom_call" | custom-call | tf_op jit(solution)/shard_map/gather/pallas_call | solution.py:927
  83.4 0.7 copy.7
Async XLA Ops:
  0.6 70.9 %copy-start = (f32[16,16,128]{2,1,0:T(8,128)S(1)}, f32[16,16,128]{2,1,0:T(8,128)}, u32[]{:S(2)}) copy-start(f32[16,16,128]{2,1,0:T(8,128)} %modulus.3) | copy-start | bytes 393220
